TPU v7x, 128 devices: a whole 4x4x4 slice. The times are simulated.
128 devices in a mesh: space: 32 (over y, x, core), chan: 4 (over z).
Axes of the slice: x: 4, y: 4, z: 4, core: 2. Of those that a mesh axis runs over, the one named last changes fastest.
Arguments:
- features: bfloat16 [256, 128, 512], P('space'), may hold values from -6 to 6
- voxel_mask: int32 [256, 512], P('space'), may hold values 0 or 1
- neighbors: int32 [256, 26], P('space'), may hold values from -1 to 15, as said below
- w_conv: bfloat16 [27, 128, 128], P(None, 'chan'), may hold values from -0.109375 to 0.109375
- w_down: bfloat16 [8, 256, 128], replicated, may hold values from -0.1875 to 0.1875
- coarse_owner: int32 [256, 1], P('space'), may hold values from 0 to 31; in each aligned block of 8 rows (0 to 7, 8 to 15, ...) at most 2 rows name the same one
- cotangent: bfloat16 [2048, 256, 64], P('space', 'chan'), may hold values from -0.25 to 0.25
Outputs:
- coarse: bfloat16 [2048, 256, 64], P('space', 'chan')
- grad_conv: float32 [27, 128, 128], P(None, 'chan')
- grad_down: float32 [8, 256, 128], P(None, 'chan')
Inputs may be any that keep to these rules, and one draw needn't show every extreme that they name: `neighbors`: blocks 0 to 3 of a device lie in the first x-layer of its slab and the others in the second; slabs follow each other along x in device order, and block positions in a layer lie on a 8 x 8 grid in y and z. An entry is the neighbor's slot on the own device (below 8), 8 + i for slot 4 + i of the previous device, 12 + i for slot i of the next device, or -1 where the position is empty. `coarse_owner`: among the 8 blocks of one device at most 2 name the same owner.
All inputs are finite; a program needn't handle non-finite values. No bound on the sum of `voxel_mask` on one device may be relied on, other than what follows from the above.
Results may differ from a plain program's by a relative error of at most 0.001.
The roundings to bfloat16 on the way count: a program that leaves them out, or rounds other values in their place, can miss the bound.
Values may be sent and summed in bfloat16 or wider, within the bound.
A program may use at most 128 MiB of HBM per device.

v0:
```python
import jax
import jax.numpy as jnp
from jax import lax
from jax.experimental import pallas as pl
from jax.experimental.pallas import tpu as pltpu
from jax.sharding import PartitionSpec as P

F32 = jnp.float32
BF16 = jnp.bfloat16
NT = (((1,), (1,)), ((), ()))
ZERO_PLANE = 72


def voxel_order():
    row = lax.broadcasted_iota(jnp.int32, (256, 256), 0)
    col = lax.broadcasted_iota(jnp.int32, (256, 256), 1)
    y = ((row >> 2) & 3) * 2 + ((row >> 5) & 1)
    z = (row & 3) * 2 + ((row >> 4) & 1)
    source = (row & ~63) + y * 8 + z
    return (source == col).astype(F32).astype(BF16)


def planes_kernel(features, mask, planes, row_mask):
    order = voxel_order()
    mine = lax.axis_index("chan") * 2

    @pl.loop(0, 8)
    def _(g):
        keep = mask[pl.ds(g, 1), :].astype(F32).astype(BF16)
        masked = features[g] * keep
        for h in range(2):
            turned = lax.dot_general(
                order, masked[:, 256 * h : 256 * h + 256], NT, preferred_element_type=F32
            )
            planes[pl.ds(8 * g + 4 * h, 4)] = turned.astype(BF16).reshape(4, 64, 128)

    for b in range(2):
        keep = mask[pl.ds(mine + b, 1), :].astype(F32)
        for h in range(2):
            wide = jnp.broadcast_to(keep[:, 256 * h : 256 * h + 256], (128, 256)).astype(BF16)
            turned = lax.dot_general(order, wide, NT, preferred_element_type=F32)
            row_mask[b, 256 * h : 256 * h + 256, :] = turned


def make_planes(features, mask):
    return pl.pallas_call(
        planes_kernel,
        out_shape=(
            jax.ShapeDtypeStruct((64, 64, 128), BF16),
            jax.ShapeDtypeStruct((2, 512, 128), F32),
        ),
    )(features, mask)


def fill_plane(windows, planes, near, b, mine, xp, sx):
    local_x = lax.rem(xp + 7, 8)
    qy = (lax.broadcasted_iota(jnp.int32, (16, 128), 0) >> 2) & 3
    qz = lax.broadcasted_iota(jnp.int32, (16, 128), 0) & 3
    loaded = {}
    for sy in (-1, 0, 1):
        for sz in (-1, 0, 1):
            position = 9 * (sx + 1) + 3 * (sy + 1) + (sz + 1)
            if position == 13:
                slot = mine + b
            else:
                slot = near[mine + b, position if position < 13 else position - 1]
            plane = jnp.where(
                slot < 0, ZERO_PLANE, jnp.where(slot < 8, 8 * slot + local_x, 56 + slot)
            )
            loaded[sy, sz] = planes[plane].astype(F32).reshape(4, 16, 128)

    def merged(oy, sz, tile):
        inner = loaded[0, sz][tile]
        if oy == 0:
            return inner
        return jnp.where(qy == (3 if oy < 0 else 0), loaded[oy, sz][tile], inner)

    def turned(value, shift):
        return value if shift % 16 == 0 else pltpu.roll(value, shift % 16, 0)

    for i in range(4):
        for j in range(4):
            oy = (-1, 0, 0, 1)[i]
            oz = (-1, 0, 0, 1)[j]
            tile = (1, 0, 1, 0)[i] * 2 + (1, 0, 1, 0)[j]
            value = turned(merged(oy, 0, tile), -4 * oy - oz)
            if oz != 0:
                edge = turned(merged(oy, oz, tile), -4 * oy + 3 * oz)
                value = jnp.where(qz == (0 if oz < 0 else 3), edge, value)
            value = value.astype(BF16)
            for p in range(2):
                for e in range(2):
                    dy, dz = i - p, j - e
                    if 0 <= dy <= 2 and 0 <= dz <= 2:
                        row = 32 * p + 16 * e
                        col = 128 * (3 * dy + dz)
                        windows[b, xp, row : row + 16, col : col + 128] = value


def block_kernel(
    near, planes, before, after, row_mask, w_conv, w_down, dpiece,
    pieces, conv_grad, down_grad,
    table, windows, octants, factor, slopes,
):
    mine = lax.axis_index("chan") * 2
    table[0:64] = planes[...]
    table[64:68] = before[...]
    table[68:72] = after[...]
    table[72] = jnp.zeros((64, 128), BF16)
    for b in range(2):
        fill_plane(windows, table, near, b, mine, 0, -1)
        fill_plane(windows, table, near, b, mine, 9, 1)

        @pl.loop(1, 9)
        def _(xp):
            fill_plane(windows, table, near, b, mine, xp, 0)

    for b in range(2):
        total = None
        for dx in range(3):
            part = lax.dot_general(
                windows[b, dx : dx + 8].reshape(512, 1152), w_conv[dx], NT,
                preferred_element_type=F32,
            )
            total = part if total is None else total + part
        own = table[pl.ds(8 * (mine + b), 8)].astype(F32).reshape(512, 128)
        pre = own + total
        keep = row_mask[b]
        gate = jax.nn.sigmoid(pre)
        hidden = (keep * (pre * gate)).astype(BF16).reshape(4, 2, 4, 16, 128)
        factor[b] = keep * gate * (1.0 + pre * (1.0 - gate))
        for a in range(2):
            for t in range(4):
                octants[4 * a + t, 64 * b : 64 * b + 64, :] = hidden[:, a, t].reshape(64, 128)
    total = None
    for o in range(8):
        part = lax.dot_general(w_down[o], octants[o], NT, preferred_element_type=F32)
        total = part if total is None else total + part
    pieces[...] = total.astype(BF16)

    piece = dpiece[...]
    piece_rows = piece.astype(F32).T.astype(BF16)
    for o in range(8):
        down_grad[o] = jnp.dot(piece, octants[o], preferred_element_type=F32)
    for b in range(2):
        for a in range(2):
            for t in range(4):
                o = 4 * a + t
                dhidden = jnp.dot(
                    piece_rows[64 * b : 64 * b + 64], w_down[o], preferred_element_type=F32
                ).reshape(4, 16, 128)
                for qx in range(4):
                    row = 64 * (2 * qx + a) + 16 * t
                    slopes[b, row : row + 16, :] = dhidden[qx] * factor[b, row : row + 16, :]
    for dx in range(3):
        total = None
        for b in range(2):
            rows = slopes[b].astype(BF16).astype(F32).T.astype(BF16)
            part = jnp.dot(
                rows, windows[b, dx : dx + 8].reshape(512, 1152), preferred_element_type=F32
            )
            total = part if total is None else total + part
        conv_grad[dx] = total


def run_blocks(near, planes, before, after, row_mask, w_conv, w_down, dpiece):
    vmem = pl.BlockSpec(memory_space=pltpu.VMEM)
    return pl.pallas_call(
        block_kernel,
        out_shape=(
            jax.ShapeDtypeStruct((256, 128), BF16),
            jax.ShapeDtypeStruct((3, 128, 1152), F32),
            jax.ShapeDtypeStruct((8, 256, 128), F32),
        ),
        in_specs=[pl.BlockSpec(memory_space=pltpu.SMEM)] + [vmem] * 7,
        out_specs=(vmem, vmem, vmem),
        scratch_shapes=[
            pltpu.VMEM((73, 64, 128), BF16),
            pltpu.VMEM((2, 10, 64, 1152), BF16),
            pltpu.VMEM((8, 128, 128), BF16),
            pltpu.VMEM((2, 512, 128), F32),
            pltpu.VMEM((2, 512, 128), F32),
        ],
        compiler_params=pltpu.CompilerParams(vmem_limit_bytes=56 << 20),
    )(near, planes, before, after, row_mask, w_conv, w_down, dpiece)


def routing_table(owner, peers, capacity):
    targets = jnp.arange(peers, dtype=jnp.int32)
    dest_hits = (owner[:, None] == targets[None, :]).astype(jnp.int32)
    earlier = jnp.cumsum(dest_hits, axis=0) - dest_hits
    dest_rank = jnp.sum(earlier * dest_hits, axis=1)
    places = jnp.arange(capacity, dtype=jnp.int32)
    return (owner[None, None, :] == targets[:, None, None]) & (
        dest_rank[None, None, :] == places[None, :, None]
    )


def local(features, voxel_mask, neighbors, w_conv, w_down, coarse_owner, cotangent):
    peers = lax.axis_size("space")
    shards = lax.axis_size("chan")
    planes, row_mask = make_planes(features, voxel_mask)
    by_block = planes.reshape(8, 8, 64, 128)
    before = lax.ppermute(by_block[4:, 7], "space", [(i, i + 1) for i in range(peers - 1)])
    after = lax.ppermute(by_block[:4, 0], "space", [(i + 1, i) for i in range(peers - 1)])
    w_rows = w_conv.reshape(3, 9, -1, 128).transpose(0, 2, 1, 3).reshape(3, -1, 1152)
    w_all = lax.all_gather(w_rows, "chan", axis=1, tiled=True)
    capacity = cotangent.shape[0] // peers
    down_width = cotangent.shape[1]
    chosen = routing_table(coarse_owner[:, 0], peers, capacity).astype(BF16)
    returned = lax.all_to_all(
        cotangent.reshape(peers, capacity, down_width, 64),
        "space", split_axis=0, concat_axis=0, tiled=True,
    )
    dpiece = jnp.einsum(
        "drj,drcq->jcq", chosen, returned, preferred_element_type=F32
    ).astype(BF16)
    dpiece = dpiece.reshape(shards, 2, down_width, 64).transpose(0, 2, 1, 3)
    dpiece = lax.all_to_all(dpiece, "chan", split_axis=0, concat_axis=0, tiled=True)
    dpiece = dpiece.reshape(shards * down_width, 128)
    pieces, conv_grad, down_grad = run_blocks(
        neighbors, planes, before, after, row_mask, w_all, w_down, dpiece
    )
    pieces = lax.all_to_all(
        pieces.reshape(shards, down_width, 128), "chan", split_axis=0, concat_axis=0, tiled=True
    )
    pieces = pieces.reshape(shards, down_width, 2, 64).transpose(0, 2, 1, 3)
    pieces = pieces.reshape(8, down_width, 64)
    outgoing = jnp.einsum(
        "drj,jcq->drcq", chosen, pieces, preferred_element_type=F32
    ).astype(BF16)
    arrived = lax.all_to_all(outgoing, "space", split_axis=0, concat_axis=0, tiled=True)
    coarse = arrived.reshape(peers * capacity, down_width, 64)
    conv_part = lax.psum_scatter(conv_grad, "chan", scatter_dimension=1, tiled=True)
    down_part = lax.psum_scatter(down_grad, "chan", scatter_dimension=1, tiled=True)
    conv_sum, down_sum = lax.psum((conv_part, down_part), "space")
    conv_sum = conv_sum.reshape(3, -1, 9, 128).transpose(0, 2, 1, 3).reshape(27, -1, 128)
    return (coarse, conv_sum, down_sum)


def solution(mesh):
    in_specs = (
        P("space", None, None),
        P("space", None),
        P("space", None),
        P(None, "chan", None),
        P(),
        P("space", None),
        P("space", "chan", None),
    )
    out_specs = (P("space", "chan", None), P(None, "chan", None), P(None, "chan", None))
    return jax.shard_map(local, mesh=mesh, in_specs=in_specs, out_specs=out_specs, check_vma=False)
```

profile of v0, /device:TPU:1, one launch (start us, length us, event | category | flops | bytes accessed | tf_op | source)
XLA Modules:
  0.0 234.9 jit_solution(11291398317957137875)
XLA Ops:
  7.2 2.3 copy.67
  9.5 1.5 reshape.103
  11.0 8.6 %all-to-all-start = ((bf16[32,2,4096]{2,1,0:T(2,128)(2,1)}), bf16[32,2,4096]{2,1,0:T(2,128)(2,1)S(1)}, u32[]{:S(2)}, u32[]{:S(2)}) async-start(bf16[32,2,4096]{2,1,0:T(2,128)(2,1)} %reshape.103), calls=%async_computation | async-start | bytes 1048576 | tf_op jit(solution)/shard_map/all_to_all | solution.py:211
  19.6 4.4 %shard_map.94 = (bf16[64,64,128]{2,1,0:T(8,128)(2,1)}, f32[2,512,128]{2,1,0:T(8,128)}) custom-call(bf16[8,128,512]{2,1,0:T(8,128)(2,1)} %features.1, s32[8,512]{1,0:T(8,128)} %mask.1), custom_call_target="tpu_custom_call" | custom-call | tf_op jit(solution)/shard_map/pallas_call | solution.py:46
  24.0 0.9 slice_bitcast_fusion
  24.9 2.1 collective-permute-start.1
  27.1 3.4 %collective-permute-start = (bf16[4,64,128]{2,1,0:T(8,128)(2,1)S(1)}, bf16[4,64,128]{2,1,0:T(8,128)(2,1)S(1)}, u32[]{:S(2)}, u32[]{:S(2)}) collective-permute-start(bf16[4,64,128]{2,1,0:T(8,128)(2,1)S(1)} %get-tuple-element.16), channel_id=1, source_target_pairs={{0,4},{4,8},{8,12},{12,16},{16,20},{20,24},{24,28},{28,32},{32,36}... | collective-permute-start | bytes 196616 | tf_op jit(solution)/shard_map/ppermute | solution.py:204
  30.7 0.1 reshape.91
  30.9 0.2 select_reduce_fusion
  31.1 0.7 reshape.104
  31.8 0.7 fusion
  32.6 0.8 reshape.105
  33.4 5.0 %all-to-all-start.1 = ((bf16[4,2,4096]{2,1,0:T(2,128)(2,1)}), bf16[4,2,4096]{2,1,0:T(2,128)(2,1)S(1)}, u32[]{:S(2)}, u32[]{:S(2)}) async-start(bf16[4,2,4096]{2,1,0:T(2,128)(2,1)} %reshape.105), calls=%async_computation.1 | async-start | bytes 131072 | tf_op jit(solution)/shard_map/all_to_all | solution.py:219
  38.4 13.2 %all_gather.3.w_conv = bf16[3,128,1152]{2,1,0:T(8,128)(2,1)} all-gather(bf16[3,32,1152]{2,1,0:T(8,128)(2,1)S(1)} %reshape.91), channel_id=1, replica_groups=mesh['space'=32,'chan'=4] {'chan'}, dimensions={1}, use_global_device_ids=true | all-gather | bytes 1105920 | tf_op jit(solution)/shard_map/all_gather | solution.py:207
  51.6 0.1 reshape.106
  51.7 0.7 reshape.94.dpiece
  52.5 0.6 copy-done.1
  53.1 8.1 %shard_map.95 = (bf16[256,128]{1,0:T(8,128)(2,1)}, f32[3,128,1152]{2,1,0:T(8,128)}, f32[8,256,128]{2,1,0:T(8,128)}) custom-call(s32[8,26]{1,0:T(8,128)} %near.1, bf16[64,64,128]{2,1,0:T(8,128)(2,1)} %get-tuple-element.8.planes, bf16[4,64,128]{2,1,0:T(8,128)(2,1)} %copy-done.2, bf16[4,64,128]{2,1,0:T(8,128)(2,1)} %copy-done.1, ...), custom_call_target="tpu_custom_call" | custom-call | tf_op jit(solution)/shard_map/pallas_call | solution.py:168
  61.3 0.7 reduce-scatter.5.cloned.1.call-update
  62.1 6.8 %all_to_all.20 = bf16[4,64,128]{2,1,0:T(8,128)(2,1)S(1)} all-to-all(bf16[4,64,128]{2,1,0:T(8,128)(2,1)S(1)} %bitcast.55), channel_id=1, replica_groups=mesh['space'=32,'chan'=4] {'chan'}, dimensions={0} | all-to-all | bytes 131072 | tf_op jit(solution)/shard_map/all_to_all | solution.py:224
  69.0 0.5 convolution_convert_fusion
  69.6 0.4 copy.48
  70.0 1.5 reshape.107
  71.5 12.0 %all-to-all-start.3 = ((bf16[32,2,4096]{2,1,0:T(2,128)(2,1)}), bf16[32,2,4096]{2,1,0:T(2,128)(2,1)S(1)}, u32[]{:S(2)}, u32[]{:S(2)}) async-start(bf16[32,2,4096]{2,1,0:T(2,128)(2,1)} %reshape.107), calls=%async_computation.3 | async-start | bytes 1048576 | tf_op jit(solution)/shard_map/all_to_all | solution.py:232
  83.6 7.7 %reduce-scatter.3.cloned.1.call-done = f32[3,32,1152]{2,1,0:T(8,128)} async-done(((f32[3,128,1152]{2,1,0:T(8,128)}), f32[3,32,1152]{2,1,0:T(8,128)}) %reduce-scatter.3.cloned.1.call-update) | async-done | bytes 442384 | tf_op jit(solution)/shard_map/reduce_scatter | solution.py:234
  91.3 1.1 reshape.98
  92.4 0.9 copy.49
  93.3 22.6 %reduce-scatter.5.cloned.1.call-done = f32[8,64,128]{2,1,0:T(8,128)} async-done(((f32[8,256,128]{2,1,0:T(8,128)}), f32[8,64,128]{2,1,0:T(8,128)}) %reduce-scatter.5.cloned.1.call-update) | async-done | bytes 262160 | tf_op jit(solution)/shard_map/reduce_scatter | solution.py:235
  115.9 1.6 reshape.108
  117.6 107.3 %all-reduce.3.cloned.1.call-done = (f32[27,32,128]{2,1,0:T(8,128)}, f32[8,64,128]{2,1,0:T(8,128)}) async-done(((f32[27,32,128]{2,1,0:T(8,128)}, f32[8,64,128]{2,1,0:T(8,128)}), (f32[27,32,128]{2,1,0:T(8,128)}, f32[8,64,128]{2,1,0:T(8,128)})) %all-reduce.3.cloned.1.call-update) | async-done | bytes 704528 | tf_op jit(solution)/shard_map/psum | solution.py:236
  224.9 1.8 copy.70
  226.7 1.7 copy.71
  (27 shorter events, 0.7 us)
Async XLA Ops:
  9.5 21.0 %copy-start.4 = (s32[8,1]{0,1:T(1,128)S(1)}, s32[8,1]{0,1:T(1,128)}, u32[]{:S(2)}) copy-start(s32[8,1]{0,1:T(1,128)} %param.12) | copy-start | bytes 100
  9.5 21.1 %copy-start = (bf16[27,32,128]{2,1,0:T(8,128)(2,1)S(1)}, bf16[27,32,128]{2,1,0:T(8,128)(2,1)}, u32[]{:S(2)}) copy-start(bf16[27,32,128]{2,1,0:T(8,128)(2,1)} %param.10) | copy-start | bytes 663556
  11.0 20.1 %all-to-all-start = ((bf16[32,2,4096]{2,1,0:T(2,128)(2,1)}), bf16[32,2,4096]{2,1,0:T(2,128)(2,1)S(1)}, u32[]{:S(2)}, u32[]{:S(2)}) async-start(bf16[32,2,4096]{2,1,0:T(2,128)(2,1)} %reshape.103), calls=%async_computation | async-start | bytes 1048576 | tf_op jit(solution)/shard_map/all_to_all | solution.py:211
  24.9 27.6 %collective-permute-start.1 = (bf16[4,64,128]{2,1,0:T(8,128)(2,1)S(1)}, bf16[4,64,128]{2,1,0:T(8,128)(2,1)S(1)}, u32[]{:S(2)}, u32[]{:S(2)}) collective-permute-start(bf16[4,64,128]{2,1,0:T(8,128)(2,1)S(1)} %get-tuple-element.15), channel_id=1, source_target_pairs={{4,0},{8,4},{12,8},{16,12},{20,16},{24,20},{28,24},{32,28},{36,32}... | collective-permute-start | bytes 196616 | tf_op jit(solution)/shard_map/ppermute | solution.py:205
  27.1 25.4 %collective-permute-start = (bf16[4,64,128]{2,1,0:T(8,128)(2,1)S(1)}, bf16[4,64,128]{2,1,0:T(8,128)(2,1)S(1)}, u32[]{:S(2)}, u32[]{:S(2)}) collective-permute-start(bf16[4,64,128]{2,1,0:T(8,128)(2,1)S(1)} %get-tuple-element.16), channel_id=1, source_target_pairs={{0,4},{4,8},{8,12},{12,16},{16,20},{20,24},{24,28},{28,32},{32,36}... | collective-permute-start | bytes 196616 | tf_op jit(solution)/shard_map/ppermute | solution.py:204
  33.4 18.2 %all-to-all-start.1 = ((bf16[4,2,4096]{2,1,0:T(2,128)(2,1)}), bf16[4,2,4096]{2,1,0:T(2,128)(2,1)S(1)}, u32[]{:S(2)}, u32[]{:S(2)}) async-start(bf16[4,2,4096]{2,1,0:T(2,128)(2,1)} %reshape.105), calls=%async_computation.1 | async-start | bytes 131072 | tf_op jit(solution)/shard_map/all_to_all | solution.py:219
  38.4 52.9 %reduce-scatter.3.cloned.1.call-start = ((), (), s32[]{:S(2)}) async-start(), calls=%async_computation.6 | async-start | bytes 2211840 | tf_op jit(solution)/shard_map/reduce_scatter | solution.py:234
  52.5 0.6 copy-start.1
  52.5 0.6 copy-start.2
  61.2 0.8 copy-start.3
  61.2 54.7 %reduce-scatter.5.cloned.1.call-start = ((), (), s32[]{:S(2)}) async-start(), calls=%async_computation.7 | async-start | bytes 1310720 | tf_op jit(solution)/shard_map/reduce_scatter | solution.py:235
  71.5 44.4 %all-to-all-start.3 = ((bf16[32,2,4096]{2,1,0:T(2,128)(2,1)}), bf16[32,2,4096]{2,1,0:T(2,128)(2,1)S(1)}, u32[]{:S(2)}, u32[]{:S(2)}) async-start(bf16[32,2,4096]{2,1,0:T(2,128)(2,1)} %reshape.107), calls=%async_computation.3 | async-start | bytes 1048576 | tf_op jit(solution)/shard_map/all_to_all | solution.py:232
  83.6 141.3 %all-reduce.3.cloned.1.call-start = ((), (), s32[]{:S(2)}) async-start(), calls=%async_computation.8 | async-start | bytes 1409024 | tf_op jit(solution)/shard_map/psum | solution.py:236
Sparse Core Ops, SparseCore 0:
  61.4 29.9 reduce-scatter.2
  93.7 22.1 reduce-scatter.4
  119.9 104.9 all-reduce.2
where the time goes:
time: 236 us; the launch traced here: 235 us
  waiting for transfers between devices  138 us (58%)
  starting transfers between devices  31.3 us (13%)
  blocking collectives  20 us (8%)
  local copies, waits for them, and re-layouts  17.2 us (7%)
  between operations  13.9 us (6%)
  Pallas kernels  12.5 us (5%)
    psum x1, waiting for transfers between devices, local(): conv_sum, down_sum = lax.psum((conv_part, down_part), 'space')  107 us
    reduce_scatter x1, waiting for transfers between devices, local(): lax.psum_scatter(down_grad, 'chan', scatter_dimension=1, tiled=True)  22.6 us
    all_gather x1, blocking collectives, local(): w_all = lax.all_gather(w_rows, 'chan', axis=1, tiled=True)  13.2 us
    all_to_all x1, starting transfers between devices, local(): lax.all_to_all(outgoing, 'space', split_axis=0, concat_axis=0, tiled=True)  12 us
    unnamed x18, local copies, waits for them, and re-layouts  10.5 us
    all_to_all x1, starting transfers between devices, local(): lax.all_to_all(cotangent.reshape(peers, capacity, down_width, 64), 'space...  8.58 us
    pallas_call x1, Pallas kernels, run_blocks(): pl.pallas_call(block_kernel, out_shape=(jax.ShapeDtypeStruct((256, 128),...  8.09 us
    reduce_scatter x1, waiting for transfers between devices, local(): lax.psum_scatter(conv_grad, 'chan', scatter_dimension=1, tiled=True)  7.73 us
  transfers between devices with their start and end apart: 8, of which 3 were waited for; matrix products, arithmetic and copies ran while one was open for 5% of the time, Pallas kernels for 2%

commit v1 on v0

--- a/solution.py
+++ b/solution.py
@@ -97,16 +97,243 @@
                         windows[b, xp, row : row + 16, col : col + 128] = value
 
 
+def grid_of(peers):
+    chips = peers // 2
+    across = 4 if chips == 16 else (2 if chips == 4 else 1)
+    return chips // across, across
+
+
+class Links:
+    def __init__(self):
+        self.ny, self.nx = grid_of(lax.axis_size("space"))
+        self.nz = lax.axis_size("chan")
+        space = lax.axis_index("space")
+        self.space = space
+        self.z = lax.axis_index("chan")
+        self.core = lax.rem(space, 2)
+        self.x = lax.rem(space // 2, self.nx)
+        self.y = space // (2 * self.nx)
+
+    def device(self, y=None, x=None, z=None, core=None):
+        y = self.y if y is None else y
+        x = self.x if x is None else x
+        z = self.z if z is None else z
+        core = self.core if core is None else core
+        return ((y * self.nx + x) * 2 + core, z)
+
+
+def send(source, target, sems, device):
+    pltpu.make_async_remote_copy(
+        src_ref=source, dst_ref=target, send_sem=sems[0], recv_sem=sems[1],
+        device_id=device, device_id_type=pl.DeviceIdType.MESH,
+    ).start()
+
+
+def arrived(ref, sems, device):
+    pltpu.make_async_remote_copy(
+        src_ref=ref, dst_ref=ref, send_sem=sems[0], recv_sem=sems[1],
+        device_id=device, device_id_type=pl.DeviceIdType.MESH,
+    ).wait_recv()
+
+
+def left(ref, sems, device):
+    pltpu.make_async_remote_copy(
+        src_ref=ref, dst_ref=ref, send_sem=sems[0], recv_sem=sems[1],
+        device_id=device, device_id_type=pl.DeviceIdType.MESH,
+    ).wait_send()
+
+
+def shifted(place, step, count):
+    return lax.rem(place + step, count)
+
+
+class Reduce:
+    def __init__(self, links, grads, pair, first, rest, second, sums, sems):
+        self.k = links
+        self.grads, self.pair, self.first, self.rest = grads, pair, first, rest
+        self.second, self.sums, self.sems = second, sums, sems
+        self.partner = links.device(core=1 - links.core)
+        k = links
+        self.major = [("z", k.nz), ("x", k.nx), ("y", k.ny)]
+        self.minor = [
+            (("y", k.ny), ("x", k.nx)), (("z", k.nz), ("y", k.ny)), (("z", k.nz), ("x", k.nx)),
+        ]
+        self.cell = 256 // (k.nx * k.ny)
+
+    def at(self, name):
+        return getattr(self.k, name)
+
+    def sem(self, phase, color):
+        return (self.sems.at[0, phase, color], self.sems.at[1, phase, color])
+
+    def start_pair(self, color):
+        away = pl.multiple_of(256 * (1 - self.k.core), 256)
+        send(
+            self.grads.at[color, :, pl.ds(away, 256)], self.pair.at[color],
+            self.sem(0, color), self.partner,
+        )
+
+    def part(self, color, place):
+        half = 256 * self.k.core
+        if color == 0:
+            return self.grads.at[color, place, pl.ds(pl.multiple_of(half, 256), 256)]
+        rows = 256 // self.major[color][1]
+        return self.grads.at[color, :, pl.ds(pl.multiple_of(half + place * rows, rows), rows)]
+
+    def start_major(self, color):
+        half = pl.ds(pl.multiple_of(256 * self.k.core, 256), 256)
+        arrived(self.pair.at[color], self.sem(0, color), self.partner)
+        for z in range(self.k.nz):
+            self.grads[color, z, half] += self.pair[color, z]
+        name, count = self.major[color]
+        for step in range(1, count):
+            place = shifted(self.at(name), step, count)
+            send(
+                self.part(color, place), self.first[color].at[step - 1],
+                self.sem(1, color), self.k.device(**{name: place}),
+            )
+
+    def start_minor(self, color):
+        name, count = self.major[color]
+        place = self.at(name)
+        if count > 1:
+            arrived(self.first[color].at[0 : count - 1], self.sem(1, color), self.partner)
+        half = 256 * self.k.core
+        if color == 0:
+            total = self.grads[0, place, pl.ds(pl.multiple_of(half, 256), 256)]
+        else:
+            rows = 256 // count
+            total = self.grads[color, :, pl.ds(pl.multiple_of(half + place * rows, rows), rows)]
+        for step in range(count - 1):
+            total = total + self.first[color][step]
+        (n0, c0), (n1, c1) = self.minor[color]
+        self.rest[color][...] = total.reshape(c0, c1, self.cell, 128)
+        for step0 in range(c0):
+            for step1 in range(c1):
+                if step0 == 0 and step1 == 0:
+                    continue
+                p0 = shifted(self.at(n0), step0, c0)
+                p1 = shifted(self.at(n1), step1, c1)
+                send(
+                    self.rest[color].at[p0, p1], self.second[color].at[step0 * c1 + step1 - 1],
+                    self.sem(2, color), self.k.device(**{n0: p0, n1: p1}),
+                )
+
+    def home(self, color):
+        k = self.k
+        inner = (k.x * k.ny + k.y) if color == 1 else (k.y * k.nx + k.x)
+        return pl.ds(pl.multiple_of(256 * k.core + inner * self.cell, self.cell), self.cell)
+
+    def start_spread(self, color):
+        k = self.k
+        (n0, c0), (n1, c1) = self.minor[color]
+        if c0 * c1 > 1:
+            arrived(self.second[color], self.sem(2, color), self.partner)
+        total = self.rest[color][self.at(n0), self.at(n1)]
+        for step in range(c0 * c1 - 1):
+            total = total + self.second[color][step]
+        self.sums[color, self.home(color)] = total
+        for step0 in range(k.ny):
+            for step1 in range(k.nx):
+                if step0 == 0 and step1 == 0:
+                    continue
+                y = shifted(k.y, step0, k.ny)
+                x = shifted(k.x, step1, k.nx)
+                mine = self.sums.at[color, self.home(color)]
+                send(mine, mine, self.sem(3, color), k.device(y=y, x=x))
+
+    def start_share(self, color):
+        k = self.k
+        others = k.nx * k.ny - 1
+        if others:
+            arrived(self.sums.at[color, 0 : others * self.cell], self.sem(3, color), self.partner)
+        half = pl.ds(pl.multiple_of(256 * k.core, 256), 256)
+        mine = self.sums.at[color, half]
+        send(mine, mine, self.sem(4, color), self.partner)
+
+    def finish(self, color):
+        k = self.k
+        arrived(self.sums.at[color, 0:256], self.sem(4, color), self.partner)
+        left(self.pair.at[color], self.sem(0, color), self.partner)
+        count = self.major[color][1]
+        if count > 1:
+            left(self.first[color].at[0 : count - 1], self.sem(1, color), self.partner)
+        if self.minor[color][0][1] * self.minor[color][1][1] > 1:
+            left(self.second[color], self.sem(2, color), self.partner)
+        others = k.nx * k.ny - 1
+        if others:
+            left(self.sums.at[color, 0 : others * self.cell], self.sem(3, color), self.partner)
+        left(self.sums.at[color, 0:256], self.sem(4, color), self.partner)
+
+
+def reduce_scratch(peers, nz):
+    ny, nx = grid_of(peers)
+    cell = 256 // (nx * ny)
+    return [
+        pltpu.VMEM((3, nz, 512, 128), F32),
+        pltpu.VMEM((3, nz, 256, 128), F32),
+        pltpu.VMEM((nz - 1, 256, 128), F32),
+        pltpu.VMEM((max(nx - 1, 1), nz, 256 // nx, 128), F32),
+        pltpu.VMEM((max(ny - 1, 1), nz, 256 // ny, 128), F32),
+        pltpu.VMEM((ny, nx, cell, 128), F32),
+        pltpu.VMEM((nz, ny, cell, 128), F32),
+        pltpu.VMEM((nz, nx, cell, 128), F32),
+        pltpu.VMEM((max(ny * nx - 1, 1), cell, 128), F32),
+        pltpu.VMEM((nz * ny - 1, cell, 128), F32),
+        pltpu.VMEM((nz * nx - 1, cell, 128), F32),
+        pltpu.VMEM((3, 512, 128), F32),
+        pltpu.SemaphoreType.DMA((2, 5, 3)),
+    ]
+
+
+def enter(links):
+    barrier = pltpu.get_barrier_semaphore()
+    k = links
+    count = 0
+    for step in range(1, k.nz):
+        z = shifted(k.z, step, k.nz)
+        for other in range(k.ny):
+            y = shifted(k.y, other, k.ny)
+            pl.semaphore_signal(
+                barrier, inc=1, device_id=k.device(y=y, z=z), device_id_type=pl.DeviceIdType.MESH
+            )
+            count += 1
+        for other in range(1, k.nx):
+            x = shifted(k.x, other, k.nx)
+            pl.semaphore_signal(
+                barrier, inc=1, device_id=k.device(x=x, z=z), device_id_type=pl.DeviceIdType.MESH
+            )
+            count += 1
+    for step in range(1, k.ny * k.nx * 2):
+        space = shifted(k.space, step, k.ny * k.nx * 2)
+        pl.semaphore_signal(
+            barrier, inc=1, device_id=(space, k.z), device_id_type=pl.DeviceIdType.MESH
+        )
+        count += 1
+    pl.semaphore_wait(barrier, count)
+
+
 def block_kernel(
     near, planes, before, after, row_mask, w_conv, w_down, dpiece,
-    pieces, conv_grad, down_grad,
+    pieces, conv_sum, down_sum,
     table, windows, octants, factor, slopes,
+    grads, pair, first_z, first_x, first_y, rest_0, rest_1, rest_2,
+    second_0, second_1, second_2, sums, sems,
 ):
+    links = Links()
+    reduce = Reduce(
+        links, grads, pair, (first_z, first_x, first_y), (rest_0, rest_1, rest_2),
+        (second_0, second_1, second_2), sums, sems,
+    )
+    enter(links)
     mine = lax.axis_index("chan") * 2
     table[0:64] = planes[...]
     table[64:68] = before[...]
     table[68:72] = after[...]
     table[72] = jnp.zeros((64, 128), BF16)
+    for z in range(4):
+        grads[1, z, 448:512] = jnp.zeros((64, 128), F32)
+        grads[2, z, 416:512] = jnp.zeros((96, 128), F32)
     for b in range(2):
         fill_plane(windows, table, near, b, mine, 0, -1)
         fill_plane(windows, table, near, b, mine, 9, 1)
@@ -141,7 +368,10 @@
     piece = dpiece[...]
     piece_rows = piece.astype(F32).T.astype(BF16)
     for o in range(8):
-        down_grad[o] = jnp.dot(piece, octants[o], preferred_element_type=F32)
+        part = jnp.dot(piece, octants[o], preferred_element_type=F32)
+        for z in range(4):
+            grads[0, z, 64 * o : 64 * o + 64, :] = part[64 * z : 64 * z + 64]
+    reduce.start_pair(0)
     for b in range(2):
         for a in range(2):
             for t in range(4):
@@ -160,7 +390,32 @@
                 rows, windows[b, dx : dx + 8].reshape(512, 1152), preferred_element_type=F32
             )
             total = part if total is None else total + part
-        conv_grad[dx] = total
+        for d in range(9):
+            k = 9 * dx + d
+            color, row = (1, 32 * k) if k < 14 else (2, 32 * (k - 14))
+            for z in range(4):
+                grads[color, z, row : row + 32, :] = total[
+                    32 * z : 32 * z + 32, 128 * d : 128 * d + 128
+                ]
+        if dx == 0:
+            reduce.start_major(0)
+        else:
+            reduce.start_pair(dx)
+    reduce.start_major(1)
+    reduce.start_major(2)
+    for color in range(3):
+        reduce.start_minor(color)
+    for color in range(3):
+        reduce.start_spread(color)
+    for color in range(3):
+        reduce.start_share(color)
+    for color in range(3):
+        reduce.finish(color)
+    for o in range(8):
+        down_sum[o] = sums[0, 64 * o : 64 * o + 64]
+    for k in range(27):
+        color, row = (1, 32 * k) if k < 14 else (2, 32 * (k - 14))
+        conv_sum[k] = sums[color, row : row + 32]
 
 
 def run_blocks(near, planes, before, after, row_mask, w_conv, w_down, dpiece):
@@ -169,8 +424,8 @@
         block_kernel,
         out_shape=(
             jax.ShapeDtypeStruct((256, 128), BF16),
-            jax.ShapeDtypeStruct((3, 128, 1152), F32),
-            jax.ShapeDtypeStruct((8, 256, 128), F32),
+            jax.ShapeDtypeStruct((27, 32, 128), F32),
+            jax.ShapeDtypeStruct((8, 64, 128), F32),
         ),
         in_specs=[pl.BlockSpec(memory_space=pltpu.SMEM)] + [vmem] * 7,
         out_specs=(vmem, vmem, vmem),
@@ -180,8 +435,11 @@
             pltpu.VMEM((8, 128, 128), BF16),
             pltpu.VMEM((2, 512, 128), F32),
             pltpu.VMEM((2, 512, 128), F32),
-        ],
-        compiler_params=pltpu.CompilerParams(vmem_limit_bytes=56 << 20),
+        ]
+        + reduce_scratch(lax.axis_size("space"), lax.axis_size("chan")),
+        compiler_params=pltpu.CompilerParams(
+            vmem_limit_bytes=56 << 20, collective_id=0, has_side_effects=True
+        ),
     )(near, planes, before, after, row_mask, w_conv, w_down, dpiece)
 
 
@@ -218,7 +476,7 @@
     dpiece = dpiece.reshape(shards, 2, down_width, 64).transpose(0, 2, 1, 3)
     dpiece = lax.all_to_all(dpiece, "chan", split_axis=0, concat_axis=0, tiled=True)
     dpiece = dpiece.reshape(shards * down_width, 128)
-    pieces, conv_grad, down_grad = run_blocks(
+    pieces, conv_sum, down_sum = run_blocks(
         neighbors, planes, before, after, row_mask, w_all, w_down, dpiece
     )
     pieces = lax.all_to_all(
@@ -231,10 +489,6 @@
     ).astype(BF16)
     arrived = lax.all_to_all(outgoing, "space", split_axis=0, concat_axis=0, tiled=True)
     coarse = arrived.reshape(peers * capacity, down_width, 64)
-    conv_part = lax.psum_scatter(conv_grad, "chan", scatter_dimension=1, tiled=True)
-    down_part = lax.psum_scatter(down_grad, "chan", scatter_dimension=1, tiled=True)
-    conv_sum, down_sum = lax.psum((conv_part, down_part), "space")
-    conv_sum = conv_sum.reshape(3, -1, 9, 128).transpose(0, 2, 1, 3).reshape(27, -1, 128)
     return (coarse, conv_sum, down_sum)
 
 

time: 236 us -> 119 us (0.50)
  waiting for transfers between devices: 138 us -> 11.4 us
  Pallas kernels: 12.5 us -> 44.9 us
  between operations: 13.9 us -> 0.79 us
  starting transfers between devices: 31.3 us -> 25.1 us
  local copies, waits for them, and re-layouts: 17.2 us -> 13.2 us
    psum x1 -> x0, waiting for transfers between devices: 107 us -> none  [local(): conv_sum, down_sum = lax.psum((conv_part, down_part), 'space')]
    pallas_call x1, Pallas kernels: 8.09 us -> 40.5 us  [run_blocks(): pl.pallas_call(block_kernel, out_shape=(jax.ShapeDtypeStruct((256, 128),...]
    reduce_scatter x2 -> x0, waiting for transfers between devices: 30.3 us -> none  [the longest x1 22.6 us: local(): lax.psum_scatter(down_grad, 'chan', scatter_dimension=1, tiled=True)]
    all_to_all x1, waiting for transfers between devices: 0.01 us -> 11.4 us  [local(): lax.all_to_all(outgoing, 'space', split_axis=0, concat_axis=0, tiled=True)]
    all_to_all x1, starting transfers between devices: 12 us -> 5.81 us  [local(): lax.all_to_all(outgoing, 'space', split_axis=0, concat_axis=0, tiled=True)]
    unnamed x18 -> x20, local copies, waits for them, and re-layouts: 10.5 us -> 8.45 us
  transfers between devices with their start and end apart: 8 -> 5, of which waited for: 3 -> 1; matrix products, arithmetic and copies ran while one was open for 5% -> 4% of each run, Pallas kernels for 2% -> 4%
where the time goes in v1:
time: 119 us; the launch traced here: 118 us
  Pallas kernels  44.9 us (38%)
  starting transfers between devices  25.1 us (21%)
  blocking collectives  20.9 us (18%)
  local copies, waits for them, and re-layouts  13.2 us (11%)
  waiting for transfers between devices  11.4 us (10%)
  matrix products  1.24 us (1%)
    pallas_call x1, Pallas kernels, run_blocks(): pl.pallas_call(block_kernel, out_shape=(jax.ShapeDtypeStruct((256, 128),...  40.5 us
    all_gather x1, blocking collectives, local(): w_all = lax.all_gather(w_rows, 'chan', axis=1, tiled=True)  13.2 us
    all_to_all x1, waiting for transfers between devices, local(): lax.all_to_all(outgoing, 'space', split_axis=0, concat_axis=0, tiled=True)  11.4 us
    all_to_all x1, starting transfers between devices, local(): lax.all_to_all(cotangent.reshape(peers, capacity, down_width, 64), 'space...  8.71 us
    unnamed x20, local copies, waits for them, and re-layouts  8.45 us
    all_to_all x1, blocking collectives, local(): lax.all_to_all(pieces.reshape(shards, down_width, 128), 'chan', split_axi...  7.74 us
    all_to_all x1, starting transfers between devices, local(): lax.all_to_all(outgoing, 'space', split_axis=0, concat_axis=0, tiled=True)  5.81 us
    all_to_all x1, starting transfers between devices, local(): lax.all_to_all(dpiece, 'chan', split_axis=0, concat_axis=0, tiled=True)  5.02 us
  transfers between devices with their start and end apart: 5, of which 1 were waited for; matrix products, arithmetic and copies ran while one was open for 4% of the time, Pallas kernels for 4%

profile of v1, /device:TPU:1, one launch (start us, length us, event | category | flops | bytes accessed | tf_op | source)
XLA Modules:
  0.0 118.0 jit_solution(16651510417658037139)
XLA Ops:
  0.6 2.3 %copy.55 = bf16[32,2,64,64]{3,1,2,0:T(2,128)(2,1)S(1)} copy(bf16[32,2,64,64]{3,2,1,0:T(8,128)(2,1)} %bitcast.46) | data formatting | bytes 1048576 | tf_op jit(solution)/shard_map/reshape | solution.py:470
  2.9 1.5 %reshape.95 = bf16[32,2,4096]{2,1,0:T(2,128)(2,1)} reshape(bf16[32,64,2,64]{3,2,1,0:T(2,128)(2,1)S(1)} %bitcast.42) | data formatting | bytes 1048576
  4.5 8.7 %all-to-all-start = ((bf16[32,2,4096]{2,1,0:T(2,128)(2,1)}), bf16[32,2,4096]{2,1,0:T(2,128)(2,1)S(1)}, u32[]{:S(2)}, u32[]{:S(2)}) async-start(bf16[32,2,4096]{2,1,0:T(2,128)(2,1)} %reshape.95), calls=%async_computation | async-start | bytes 1048576 | tf_op jit(solution)/shard_map/all_to_all | solution.py:469
  13.2 4.4 %shard_map.94 = (bf16[64,64,128]{2,1,0:T(8,128)(2,1)}, f32[2,512,128]{2,1,0:T(8,128)}) custom-call(bf16[8,128,512]{2,1,0:T(8,128)(2,1)} %features.1, s32[8,512]{1,0:T(8,128)} %mask.1), custom_call_target="tpu_custom_call" | custom-call | tf_op jit(solution)/shard_map/pallas_call | solution.py:46
  17.6 0.9 slice_bitcast_fusion
  18.5 2.1 %collective-permute-start.1 = (bf16[4,64,128]{2,1,0:T(8,128)(2,1)S(1)}, bf16[4,64,128]{2,1,0:T(8,128)(2,1)S(1)}, u32[]{:S(2)}, u32[]{:S(2)}) collective-permute-start(bf16[4,64,128]{2,1,0:T(8,128)(2,1)S(1)} %get-tuple-element.13), channel_id=1, source_target_pairs={{4,0},{8,4},{12,8},{16,12},{20,16},{24,20},{28,24},{32,28},{36,32}... | collective-permute-start | bytes 196616 | tf_op jit(solution)/shard_map/ppermute | solution.py:463
  20.7 3.4 %collective-permute-start = (bf16[4,64,128]{2,1,0:T(8,128)(2,1)S(1)}, bf16[4,64,128]{2,1,0:T(8,128)(2,1)S(1)}, u32[]{:S(2)}, u32[]{:S(2)}) collective-permute-start(bf16[4,64,128]{2,1,0:T(8,128)(2,1)S(1)} %get-tuple-element.14), channel_id=1, source_target_pairs={{0,4},{4,8},{8,12},{12,16},{16,20},{20,24},{24,28},{28,32},{32,36}... | collective-permute-start | bytes 196616 | tf_op jit(solution)/shard_map/ppermute | solution.py:462
  24.1 0.1 fusion.4
  24.2 0.1 copy.53
  24.3 0.1 reshape.85
  24.4 0.2 select_reduce_fusion
  24.6 0.1 iota_compare_fusion.1
  24.7 0.7 reshape.96
  25.4 0.7 fusion
  26.1 0.1 copy.54
  26.2 0.8 reshape.97
  27.0 5.0 %all-to-all-start.1 = ((bf16[4,2,4096]{2,1,0:T(2,128)(2,1)}), bf16[4,2,4096]{2,1,0:T(2,128)(2,1)S(1)}, u32[]{:S(2)}, u32[]{:S(2)}) async-start(bf16[4,2,4096]{2,1,0:T(2,128)(2,1)} %reshape.97), calls=%async_computation.1 | async-start | bytes 131072 | tf_op jit(solution)/shard_map/all_to_all | solution.py:477
  32.0 13.2 %all_gather.3.w_conv = bf16[3,128,1152]{2,1,0:T(8,128)(2,1)} all-gather(bf16[3,32,1152]{2,1,0:T(8,128)(2,1)S(1)} %reshape.85), channel_id=1, replica_groups=mesh['space'=32,'chan'=4] {'chan'}, dimensions={1}, use_global_device_ids=true | all-gather | bytes 1105920 | tf_op jit(solution)/shard_map/all_gather | solution.py:465
  45.2 0.1 reshape.98
  45.3 0.7 reshape.88.dpiece
  46.1 0.6 copy-done.3
  46.7 40.5 %shard_map.95 = (bf16[256,128]{1,0:T(8,128)(2,1)}, f32[27,32,128]{2,1,0:T(8,128)}, f32[8,64,128]{2,1,0:T(8,128)}) custom-call(s32[8,26]{1,0:T(8,128)} %near.1, bf16[64,64,128]{2,1,0:T(8,128)(2,1)} %get-tuple-element.8.planes, bf16[4,64,128]{2,1,0:T(8,128)(2,1)} %copy-done.4, bf16[4,64,128]{2,1,0:T(8,128)(2,1)} %copy-done.3, ...), custom_call_target="tpu_custom_call" | custom-call | tf_op jit(solution)/shard_map/pallas_call | solution.py:423
  87.3 7.7 %all_to_all.20 = bf16[4,64,128]{2,1,0:T(8,128)(2,1)S(1)} all-to-all(bf16[4,64,128]{2,1,0:T(8,128)(2,1)} %bitcast.51), channel_id=1, replica_groups=mesh['space'=32,'chan'=4] {'chan'}, dimensions={0} | all-to-all | bytes 131072 | tf_op jit(solution)/shard_map/all_to_all | solution.py:482
  95.0 0.1 fusion.9
  95.1 0.5 convolution_convert_fusion
  95.7 0.4 copy.37
  96.1 1.5 %reshape.99 = bf16[32,2,4096]{2,1,0:T(2,128)(2,1)} reshape(bf16[32,2,64,64]{3,2,1,0:T(8,128)(2,1)S(1)} %copy.37) | data formatting | bytes 1048576
  97.6 5.8 %all-to-all-start.3 = ((bf16[32,2,4096]{2,1,0:T(2,128)(2,1)}), bf16[32,2,4096]{2,1,0:T(2,128)(2,1)S(1)}, u32[]{:S(2)}, u32[]{:S(2)}) async-start(bf16[32,2,4096]{2,1,0:T(2,128)(2,1)} %reshape.99), calls=%async_computation.3 | async-start | bytes 1048576 | tf_op jit(solution)/shard_map/all_to_all | solution.py:490
  103.5 11.4 %all-to-all-done.3 = bf16[32,2,4096]{2,1,0:T(2,128)(2,1)S(1)} async-done(((bf16[32,2,4096]{2,1,0:T(2,128)(2,1)}), bf16[32,2,4096]{2,1,0:T(2,128)(2,1)S(1)}, u32[]{:S(2)}, u32[]{:S(2)}) %all-to-all-start.3) | async-done | bytes 524320 | tf_op jit(solution)/shard_map/all_to_all | solution.py:490
  114.9 1.6 %reshape.100 = bf16[32,2,64,64]{3,2,1,0:T(8,128)(2,1)} reshape(bf16[32,2,4096]{2,1,0:T(2,128)(2,1)S(1)} %all-to-all-done.3) | data formatting | bytes 1048576
  116.5 0.8 copy.58
  117.3 0.7 copy.59
  (18 shorter events, 0.1 us)
Async XLA Ops:
  4.5 19.6 %copy-start.5 = (s32[8,1]{0,1:T(1,128)S(1)}, s32[8,1]{0,1:T(1,128)}, u32[]{:S(2)}) copy-start(s32[8,1]{0,1:T(1,128)} %param.12) | copy-start | bytes 100
  4.5 19.7 %copy-start.2 = (bf16[27,32,128]{2,1,0:T(8,128)(2,1)S(1)}, bf16[27,32,128]{2,1,0:T(8,128)(2,1)}, u32[]{:S(2)}) copy-start(bf16[27,32,128]{2,1,0:T(8,128)(2,1)} %param.10) | copy-start | bytes 663556
  4.5 20.2 %all-to-all-start = ((bf16[32,2,4096]{2,1,0:T(2,128)(2,1)}), bf16[32,2,4096]{2,1,0:T(2,128)(2,1)S(1)}, u32[]{:S(2)}, u32[]{:S(2)}) async-start(bf16[32,2,4096]{2,1,0:T(2,128)(2,1)} %reshape.95), calls=%async_computation | async-start | bytes 1048576 | tf_op jit(solution)/shard_map/all_to_all | solution.py:469
  18.5 27.6 %collective-permute-start.1 = (bf16[4,64,128]{2,1,0:T(8,128)(2,1)S(1)}, bf16[4,64,128]{2,1,0:T(8,128)(2,1)S(1)}, u32[]{:S(2)}, u32[]{:S(2)}) collective-permute-start(bf16[4,64,128]{2,1,0:T(8,128)(2,1)S(1)} %get-tuple-element.13), channel_id=1, source_target_pairs={{4,0},{8,4},{12,8},{16,12},{20,16},{24,20},{28,24},{32,28},{36,32}... | collective-permute-start | bytes 196616 | tf_op jit(solution)/shard_map/ppermute | solution.py:463
  20.7 25.4 %collective-permute-start = (bf16[4,64,128]{2,1,0:T(8,128)(2,1)S(1)}, bf16[4,64,128]{2,1,0:T(8,128)(2,1)S(1)}, u32[]{:S(2)}, u32[]{:S(2)}) collective-permute-start(bf16[4,64,128]{2,1,0:T(8,128)(2,1)S(1)} %get-tuple-element.14), channel_id=1, source_target_pairs={{0,4},{4,8},{8,12},{12,16},{16,20},{20,24},{24,28},{28,32},{32,36}... | collective-permute-start | bytes 196616 | tf_op jit(solution)/shard_map/ppermute | solution.py:462
  27.0 18.2 %all-to-all-start.1 = ((bf16[4,2,4096]{2,1,0:T(2,128)(2,1)}), bf16[4,2,4096]{2,1,0:T(2,128)(2,1)S(1)}, u32[]{:S(2)}, u32[]{:S(2)}) async-start(bf16[4,2,4096]{2,1,0:T(2,128)(2,1)} %reshape.97), calls=%async_computation.1 | async-start | bytes 131072 | tf_op jit(solution)/shard_map/all_to_all | solution.py:477
  46.1 0.6 copy-start.3
  46.1 0.6 copy-start.4
  97.6 17.2 %all-to-all-start.3 = ((bf16[32,2,4096]{2,1,0:T(2,128)(2,1)}), bf16[32,2,4096]{2,1,0:T(2,128)(2,1)S(1)}, u32[]{:S(2)}, u32[]{:S(2)}) async-start(bf16[32,2,4096]{2,1,0:T(2,128)(2,1)} %reshape.99), calls=%async_computation.3 | async-start | bytes 1048576 | tf_op jit(solution)/shard_map/all_to_all | solution.py:490
  103.4 13.1 %copy-start = (f32[27,32,128]{2,1,0:T(8,128)S(1)}, f32[27,32,128]{2,1,0:T(8,128)}, u32[]{:S(2)}) copy-start(f32[27,32,128]{2,1,0:T(8,128)} %get-tuple-element.21) | copy-start | bytes 1327108
  103.5 13.8 %copy-start.1 = (f32[8,64,128]{2,1,0:T(8,128)S(1)}, f32[8,64,128]{2,1,0:T(8,128)}, u32[]{:S(2)}) copy-start(f32[8,64,128]{2,1,0:T(8,128)} %get-tuple-element.22) | copy-start | bytes 786436

commit v2 on v1

--- a/solution.py
+++ b/solution.py
@@ -8,7 +8,6 @@
 F32 = jnp.float32
 BF16 = jnp.bfloat16
 NT = (((1,), (1,)), ((), ()))
-ZERO_PLANE = 72
 
 
 def voxel_order():
@@ -20,40 +19,7 @@
     return (source == col).astype(F32).astype(BF16)
 
 
-def planes_kernel(features, mask, planes, row_mask):
-    order = voxel_order()
-    mine = lax.axis_index("chan") * 2
-
-    @pl.loop(0, 8)
-    def _(g):
-        keep = mask[pl.ds(g, 1), :].astype(F32).astype(BF16)
-        masked = features[g] * keep
-        for h in range(2):
-            turned = lax.dot_general(
-                order, masked[:, 256 * h : 256 * h + 256], NT, preferred_element_type=F32
-            )
-            planes[pl.ds(8 * g + 4 * h, 4)] = turned.astype(BF16).reshape(4, 64, 128)
-
-    for b in range(2):
-        keep = mask[pl.ds(mine + b, 1), :].astype(F32)
-        for h in range(2):
-            wide = jnp.broadcast_to(keep[:, 256 * h : 256 * h + 256], (128, 256)).astype(BF16)
-            turned = lax.dot_general(order, wide, NT, preferred_element_type=F32)
-            row_mask[b, 256 * h : 256 * h + 256, :] = turned
-
-
-def make_planes(features, mask):
-    return pl.pallas_call(
-        planes_kernel,
-        out_shape=(
-            jax.ShapeDtypeStruct((64, 64, 128), BF16),
-            jax.ShapeDtypeStruct((2, 512, 128), F32),
-        ),
-    )(features, mask)
-
-
 def fill_plane(windows, planes, near, b, mine, xp, sx):
-    local_x = lax.rem(xp + 7, 8)
     qy = (lax.broadcasted_iota(jnp.int32, (16, 128), 0) >> 2) & 3
     qz = lax.broadcasted_iota(jnp.int32, (16, 128), 0) & 3
     loaded = {}
@@ -64,9 +30,10 @@
                 slot = mine + b
             else:
                 slot = near[mine + b, position if position < 13 else position - 1]
-            plane = jnp.where(
-                slot < 0, ZERO_PLANE, jnp.where(slot < 8, 8 * slot + local_x, 56 + slot)
-            )
+            if sx == 0:
+                plane = jnp.where((slot < 0) | (slot > 7), 64, 8 * slot + xp - 1)
+            else:
+                plane = jnp.where(slot < 0, 16, slot)
             loaded[sy, sz] = planes[plane].astype(F32).reshape(4, 16, 128)
 
     def merged(oy, sz, tile):
@@ -286,61 +253,161 @@
     ]
 
 
-def enter(links):
+def signal_all(links):
     barrier = pltpu.get_barrier_semaphore()
     k = links
-    count = 0
+    targets = []
     for step in range(1, k.nz):
         z = shifted(k.z, step, k.nz)
         for other in range(k.ny):
-            y = shifted(k.y, other, k.ny)
-            pl.semaphore_signal(
-                barrier, inc=1, device_id=k.device(y=y, z=z), device_id_type=pl.DeviceIdType.MESH
-            )
-            count += 1
+            targets.append(k.device(y=shifted(k.y, other, k.ny), z=z))
         for other in range(1, k.nx):
-            x = shifted(k.x, other, k.nx)
-            pl.semaphore_signal(
-                barrier, inc=1, device_id=k.device(x=x, z=z), device_id_type=pl.DeviceIdType.MESH
-            )
-            count += 1
+            targets.append(k.device(x=shifted(k.x, other, k.nx), z=z))
     for step in range(1, k.ny * k.nx * 2):
-        space = shifted(k.space, step, k.ny * k.nx * 2)
+        targets.append((shifted(k.space, step, k.ny * k.nx * 2), k.z))
+    for target in targets:
         pl.semaphore_signal(
-            barrier, inc=1, device_id=(space, k.z), device_id_type=pl.DeviceIdType.MESH
+            barrier, inc=1, device_id=target, device_id_type=pl.DeviceIdType.MESH
         )
-        count += 1
-    pl.semaphore_wait(barrier, count)
-
-
-def block_kernel(
-    near, planes, before, after, row_mask, w_conv, w_down, dpiece,
-    pieces, conv_sum, down_sum,
-    table, windows, octants, factor, slopes,
+    return barrier, len(targets)
+
+
+def start_exchange(links, source, target, sems):
+    peers = links.ny * links.nx * 2
+    for step in range(1, peers):
+        place = shifted(links.space, step, peers)
+        send(source.at[place], target.at[links.space], sems, (place, links.z))
+    target[links.space] = source[links.space]
+
+
+def start_columns(links, source, target, sems):
+    for step in range(1, links.nz):
+        place = shifted(links.z, step, links.nz)
+        send(source.at[place], target.at[links.z], sems, (links.space, place))
+    target[links.z] = source[links.z]
+
+
+def step_kernel(
+    near, owner, features_hbm, mask_hbm, w_conv_hbm, w_down_hbm, cotangent_hbm,
+    coarse_hbm, conv_sum, down_sum,
+    features, mask, w_own, w_down, cotangent, w_conv,
+    table, rims, windows, octants, factor, slopes, row_mask,
+    cot_out, cot_in, piece_out, piece_in, dpiece_out, dpiece_in,
+    halves, coarse_out, coarse_in, coarse, local_sems, front_sems,
     grads, pair, first_z, first_x, first_y, rest_0, rest_1, rest_2,
     second_0, second_1, second_2, sums, sems,
 ):
     links = Links()
+    peers = links.ny * links.nx * 2
+    nz = links.nz
+    partner = links.device(core=1 - links.core)
+    mine = links.z * 2
     reduce = Reduce(
         links, grads, pair, (first_z, first_x, first_y), (rest_0, rest_1, rest_2),
         (second_0, second_1, second_2), sums, sems,
     )
-    enter(links)
-    mine = lax.axis_index("chan") * 2
-    table[0:64] = planes[...]
-    table[64:68] = before[...]
-    table[68:72] = after[...]
-    table[72] = jnp.zeros((64, 128), BF16)
-    for z in range(4):
+
+    def front(n):
+        return (front_sems.at[0, n], front_sems.at[1, n])
+
+    loads = [
+        pltpu.make_async_copy(source, target, local_sems.at[n])
+        for n, (source, target) in enumerate(
+            (
+                (w_conv_hbm, w_own), (cotangent_hbm, cotangent), (mask_hbm, mask),
+                (features_hbm, features), (w_down_hbm, w_down),
+            )
+        )
+    ]
+    for load in loads:
+        load.start()
+    barrier, signals = signal_all(links)
+    order = voxel_order()
+
+    table[64] = jnp.zeros((64, 128), BF16)
+    rims[0, 12:17] = jnp.zeros((5, 64, 128), BF16)
+    rims[1, 8:12] = jnp.zeros((4, 64, 128), BF16)
+    rims[1, 16] = jnp.zeros((64, 128), BF16)
+    for z in range(nz):
         grads[1, z, 448:512] = jnp.zeros((64, 128), F32)
         grads[2, z, 416:512] = jnp.zeros((96, 128), F32)
+    for r in range(2):
+        halves[r, 8] = jnp.zeros((64, 128), BF16)
+    loads[0].wait()
+    for k in range(27):
+        dx, d = k // 9, k % 9
+        rows = pl.ds(pl.multiple_of(32 * links.z, 32), 32)
+        w_conv[dx, rows, 128 * d : 128 * d + 128] = w_own[k]
+    loads[1].wait()
+
+    @pl.loop(0, peers)
+    def _(d):
+        cot_out[d, :, 0:64] = cotangent[2 * d]
+        cot_out[d, :, 64:128] = cotangent[2 * d + 1]
+
+    pl.semaphore_wait(barrier, signals)
+    for step in range(1, nz):
+        z = shifted(links.z, step, nz)
+        rows = pl.ds(pl.multiple_of(32 * links.z + 16 * links.core, 16), 16)
+        send(
+            w_conv.at[:, rows], w_conv.at[:, rows],
+            (front_sems.at[0, 5 + step], front_sems.at[1, 5 + step]), links.device(z=z),
+        )
+    start_exchange(links, cot_out, cot_in, front(0))
+
+    loads[2].wait()
+    loads[3].wait()
+
+    @pl.loop(0, 8)
+    def _(g):
+        keep = mask[pl.ds(g, 1), :].astype(F32).astype(BF16)
+        masked = features[g] * keep
+        for h in range(2):
+            turned = lax.dot_general(
+                order, masked[:, 256 * h : 256 * h + 256], NT, preferred_element_type=F32
+            )
+            table[pl.ds(8 * g + 4 * h, 4)] = turned.astype(BF16).reshape(4, 64, 128)
+
+    following = (shifted(links.space, 1, peers), links.z)
+    previous = (shifted(links.space, peers - 1, peers), links.z)
+    for j in range(8):
+        rims[0, j] = table[8 * j + 7]
+        rims[1, j] = table[8 * j]
+    send(rims.at[0, 4:8], rims.at[0, 8:12], front(1), following)
+    send(rims.at[1, 0:4], rims.at[1, 12:16], front(2), previous)
     for b in range(2):
-        fill_plane(windows, table, near, b, mine, 0, -1)
-        fill_plane(windows, table, near, b, mine, 9, 1)
+        keep = mask[pl.ds(mine + b, 1), :].astype(F32)
+        for h in range(2):
+            wide = jnp.broadcast_to(keep[:, 256 * h : 256 * h + 256], (128, 256)).astype(BF16)
+            turned = lax.dot_general(order, wide, NT, preferred_element_type=F32)
+            row_mask[b, 256 * h : 256 * h + 256, :] = turned
 
         @pl.loop(1, 9)
         def _(xp):
             fill_plane(windows, table, near, b, mine, xp, 0)
+
+    for step in range(1, nz):
+        z = shifted(links.z, nz - step, nz)
+        rows = pl.ds(pl.multiple_of(32 * z + 16 * links.core, 16), 16)
+        piece = w_conv.at[:, rows]
+        arrived(piece, (front_sems.at[0, 5 + step], front_sems.at[1, 5 + step]), partner)
+        send(piece, piece, front(3), partner)
+    arrived(rims.at[0, 8:12], front(1), previous)
+    arrived(rims.at[1, 12:16], front(2), following)
+
+    @pl.when(links.space == 0)
+    def _():
+        rims[0, 8:12] = jnp.zeros((4, 64, 128), BF16)
+
+    @pl.when(links.space == peers - 1)
+    def _():
+        rims[1, 12:16] = jnp.zeros((4, 64, 128), BF16)
+
+    for b in range(2):
+        fill_plane(windows, rims.at[0], near, b, mine, 0, -1)
+        fill_plane(windows, rims.at[1], near, b, mine, 9, 1)
+    shared = w_conv.at[:, 0 : 16 * (nz - 1)]
+    arrived(shared, front(3), partner)
 
     for b in range(2):
         total = None
@@ -359,13 +426,51 @@
         for a in range(2):
             for t in range(4):
                 octants[4 * a + t, 64 * b : 64 * b + 64, :] = hidden[:, a, t].reshape(64, 128)
+    loads[4].wait()
     total = None
     for o in range(8):
         part = lax.dot_general(w_down[o], octants[o], NT, preferred_element_type=F32)
         total = part if total is None else total + part
-    pieces[...] = total.astype(BF16)
-
-    piece = dpiece[...]
+    piece_out[...] = total.astype(BF16).reshape(nz, 64, 128)
+    start_columns(links, piece_out, piece_in, front(4))
+
+    arrived(cot_in.at[0 : peers - 1], front(0), partner)
+    owners = [owner[g, 0] for g in range(8)]
+    low = lax.broadcasted_iota(jnp.int32, (64, 128), 1) < 64
+    for z in range(4):
+        parts = []
+        for i in range(2):
+            g = 2 * z + i
+            rank = jnp.int32(0)
+            for h in range(g):
+                rank = rank + jnp.where(owners[h] == owners[g], 1, 0)
+            value = cot_in[owners[g]].astype(F32)
+            parts.append(jnp.where(rank == i, value, pltpu.roll(value, 64, 1)))
+        dpiece_out[z] = jnp.where(low, parts[0], parts[1]).astype(BF16)
+    start_columns(links, dpiece_out, dpiece_in, front(5))
+
+    arrived(piece_in.at[0 : nz - 1], front(4), partner)
+    for g in range(8):
+        value = piece_in[g // 2].astype(F32)
+        swapped = pltpu.roll(value, 64, 1)
+        first, other = (value, swapped) if g % 2 == 0 else (swapped, value)
+        halves[0, g] = jnp.where(low, first, 0.0).astype(BF16)
+        halves[1, g] = jnp.where(low, 0.0, other).astype(BF16)
+
+    @pl.loop(0, peers)
+    def _(d):
+        place_0 = jnp.int32(8)
+        place_1 = jnp.int32(8)
+        for g in range(7, -1, -1):
+            hit = owners[g] == d
+            place_1 = jnp.where(hit, place_0, place_1)
+            place_0 = jnp.where(hit, g, place_0)
+        coarse_out[d] = halves[0, place_0] + halves[1, place_1]
+
+    start_exchange(links, coarse_out, coarse_in, front(9))
+
+    arrived(dpiece_in.at[0 : nz - 1], front(5), partner)
+    piece = dpiece_in[...].reshape(256, 128)
     piece_rows = piece.astype(F32).T.astype(BF16)
     for o in range(8):
         part = jnp.dot(piece, octants[o], preferred_element_type=F32)
@@ -382,12 +487,12 @@
                 for qx in range(4):
                     row = 64 * (2 * qx + a) + 16 * t
                     slopes[b, row : row + 16, :] = dhidden[qx] * factor[b, row : row + 16, :]
+    turned = [slopes[b].astype(BF16).astype(F32).T.astype(BF16) for b in range(2)]
     for dx in range(3):
         total = None
         for b in range(2):
-            rows = slopes[b].astype(BF16).astype(F32).T.astype(BF16)
             part = jnp.dot(
-                rows, windows[b, dx : dx + 8].reshape(512, 1152), preferred_element_type=F32
+                turned[b], windows[b, dx : dx + 8].reshape(512, 1152), preferred_element_type=F32
             )
             total = part if total is None else total + part
         for d in range(9):
@@ -407,6 +512,16 @@
         reduce.start_minor(color)
     for color in range(3):
         reduce.start_spread(color)
+
+    arrived(coarse_in.at[0 : peers - 1], front(9), partner)
+
+    @pl.loop(0, peers)
+    def _(d):
+        coarse[2 * d] = coarse_in[d, :, 0:64]
+        coarse[2 * d + 1] = coarse_in[d, :, 64:128]
+
+    store = pltpu.make_async_copy(coarse, coarse_hbm, local_sems.at[5])
+    store.start()
     for color in range(3):
         reduce.start_share(color)
     for color in range(3):
@@ -416,80 +531,68 @@
     for k in range(27):
         color, row = (1, 32 * k) if k < 14 else (2, 32 * (k - 14))
         conv_sum[k] = sums[color, row : row + 32]
-
-
-def run_blocks(near, planes, before, after, row_mask, w_conv, w_down, dpiece):
+    left(cot_out.at[0 : peers - 1], front(0), partner)
+    left(rims.at[0, 4:8], front(1), partner)
+    left(rims.at[1, 0:4], front(2), partner)
+    left(shared, front(3), partner)
+    left(piece_out.at[0 : nz - 1], front(4), partner)
+    left(dpiece_out.at[0 : nz - 1], front(5), partner)
+    for step in range(1, nz):
+        left(
+            w_conv.at[:, 0:16],
+            (front_sems.at[0, 5 + step], front_sems.at[1, 5 + step]), partner,
+        )
+    left(coarse_out.at[0 : peers - 1], front(9), partner)
+    store.wait()
+
+
+def local(features, voxel_mask, neighbors, w_conv, w_down, coarse_owner, cotangent):
+    peers = lax.axis_size("space")
+    nz = lax.axis_size("chan")
     vmem = pl.BlockSpec(memory_space=pltpu.VMEM)
+    smem = pl.BlockSpec(memory_space=pltpu.SMEM)
+    anywhere = pl.BlockSpec(memory_space=pl.ANY)
     return pl.pallas_call(
-        block_kernel,
+        step_kernel,
         out_shape=(
-            jax.ShapeDtypeStruct((256, 128), BF16),
+            jax.ShapeDtypeStruct(cotangent.shape, BF16),
             jax.ShapeDtypeStruct((27, 32, 128), F32),
             jax.ShapeDtypeStruct((8, 64, 128), F32),
         ),
-        in_specs=[pl.BlockSpec(memory_space=pltpu.SMEM)] + [vmem] * 7,
-        out_specs=(vmem, vmem, vmem),
+        in_specs=[smem, smem] + [anywhere] * 5,
+        out_specs=(anywhere, vmem, vmem),
         scratch_shapes=[
-            pltpu.VMEM((73, 64, 128), BF16),
+            pltpu.VMEM((8, 128, 512), BF16),
+            pltpu.VMEM((8, 512), jnp.int32),
+            pltpu.VMEM((27, 32, 128), BF16),
+            pltpu.VMEM((8, 256, 128), BF16),
+            pltpu.VMEM(cotangent.shape, BF16),
+            pltpu.VMEM((3, 128, 1152), BF16),
+            pltpu.VMEM((65, 64, 128), BF16),
+            pltpu.VMEM((2, 17, 64, 128), BF16),
             pltpu.VMEM((2, 10, 64, 1152), BF16),
             pltpu.VMEM((8, 128, 128), BF16),
             pltpu.VMEM((2, 512, 128), F32),
             pltpu.VMEM((2, 512, 128), F32),
+            pltpu.VMEM((2, 512, 128), F32),
+            pltpu.VMEM((peers, 64, 128), BF16),
+            pltpu.VMEM((peers, 64, 128), BF16),
+            pltpu.VMEM((nz, 64, 128), BF16),
+            pltpu.VMEM((nz, 64, 128), BF16),
+            pltpu.VMEM((nz, 64, 128), BF16),
+            pltpu.VMEM((nz, 64, 128), BF16),
+            pltpu.VMEM((2, 9, 64, 128), BF16),
+            pltpu.VMEM((peers, 64, 128), BF16),
+            pltpu.VMEM((peers, 64, 128), BF16),
+            pltpu.VMEM(cotangent.shape, BF16),
+            pltpu.SemaphoreType.DMA((6,)),
+            pltpu.SemaphoreType.DMA((2, 10)),
         ]
-        + reduce_scratch(lax.axis_size("space"), lax.axis_size("chan")),
+        + reduce_scratch(peers, nz),
         compiler_params=pltpu.CompilerParams(
             vmem_limit_bytes=56 << 20, collective_id=0, has_side_effects=True
         ),
-    )(near, planes, before, after, row_mask, w_conv, w_down, dpiece)
-
-
-def routing_table(owner, peers, capacity):
-    targets = jnp.arange(peers, dtype=jnp.int32)
-    dest_hits = (owner[:, None] == targets[None, :]).astype(jnp.int32)
-    earlier = jnp.cumsum(dest_hits, axis=0) - dest_hits
-    dest_rank = jnp.sum(earlier * dest_hits, axis=1)
-    places = jnp.arange(capacity, dtype=jnp.int32)
-    return (owner[None, None, :] == targets[:, None, None]) & (
-        dest_rank[None, None, :] == places[None, :, None]
-    )
-
-
-def local(features, voxel_mask, neighbors, w_conv, w_down, coarse_owner, cotangent):
-    peers = lax.axis_size("space")
-    shards = lax.axis_size("chan")
-    planes, row_mask = make_planes(features, voxel_mask)
-    by_block = planes.reshape(8, 8, 64, 128)
-    before = lax.ppermute(by_block[4:, 7], "space", [(i, i + 1) for i in range(peers - 1)])
-    after = lax.ppermute(by_block[:4, 0], "space", [(i + 1, i) for i in range(peers - 1)])
-    w_rows = w_conv.reshape(3, 9, -1, 128).transpose(0, 2, 1, 3).reshape(3, -1, 1152)
-    w_all = lax.all_gather(w_rows, "chan", axis=1, tiled=True)
-    capacity = cotangent.shape[0] // peers
-    down_width = cotangent.shape[1]
-    chosen = routing_table(coarse_owner[:, 0], peers, capacity).astype(BF16)
-    returned = lax.all_to_all(
-        cotangent.reshape(peers, capacity, down_width, 64),
-        "space", split_axis=0, concat_axis=0, tiled=True,
-    )
-    dpiece = jnp.einsum(
-        "drj,drcq->jcq", chosen, returned, preferred_element_type=F32
-    ).astype(BF16)
-    dpiece = dpiece.reshape(shards, 2, down_width, 64).transpose(0, 2, 1, 3)
-    dpiece = lax.all_to_all(dpiece, "chan", split_axis=0, concat_axis=0, tiled=True)
-    dpiece = dpiece.reshape(shards * down_width, 128)
-    pieces, conv_sum, down_sum = run_blocks(
-        neighbors, planes, before, after, row_mask, w_all, w_down, dpiece
-    )
-    pieces = lax.all_to_all(
-        pieces.reshape(shards, down_width, 128), "chan", split_axis=0, concat_axis=0, tiled=True
-    )
-    pieces = pieces.reshape(shards, down_width, 2, 64).transpose(0, 2, 1, 3)
-    pieces = pieces.reshape(8, down_width, 64)
-    outgoing = jnp.einsum(
-        "drj,jcq->drcq", chosen, pieces, preferred_element_type=F32
-    ).astype(BF16)
-    arrived = lax.all_to_all(outgoing, "space", split_axis=0, concat_axis=0, tiled=True)
-    coarse = arrived.reshape(peers * capacity, down_width, 64)
-    return (coarse, conv_sum, down_sum)
+    )(neighbors, coarse_owner, features, voxel_mask, w_conv, w_down, cotangent)
 
 
 def solution(mesh):

time: 119 us -> 60.5 us (0.51)
  starting transfers between devices: 25.1 us -> 0 us
  blocking collectives: 20.9 us -> 0 us
  waiting for transfers between devices: 11.4 us -> 0 us
  Pallas kernels: 44.9 us -> 54.2 us
  local copies, waits for them, and re-layouts: 13.2 us -> 5.44 us
  matrix products: 1.24 us -> 0 us
    all_to_all x3 -> x0, starting transfers between devices: 19.5 us -> none  [the longest x1 8.71 us: local(): lax.all_to_all(cotangent.reshape(peers, capacity, down_width, 64), 'space...]
    all_gather x1 -> x0, blocking collectives: 13.2 us -> none  [local(): w_all = lax.all_gather(w_rows, 'chan', axis=1, tiled=True)]
    all_to_all x3 -> x0, waiting for transfers between devices: 11.4 us -> none  [the longest x1 11.4 us: local(): lax.all_to_all(outgoing, 'space', split_axis=0, concat_axis=0, tiled=True)]
    pallas_call x2 -> x1, Pallas kernels: 44.9 us -> 54.2 us  [local(): pl.pallas_call(step_kernel, out_shape=(jax.ShapeDtypeStruct(cotangent.sha...]
    all_to_all x1 -> x0, blocking collectives: 7.74 us -> none  [local(): lax.all_to_all(pieces.reshape(shards, down_width, 128), 'chan', split_axi...]
    ppermute x2 -> x0, starting transfers between devices: 5.56 us -> none  [the longest x1 3.42 us: local(): lax.ppermute(by_block[4:, 7], 'space', [(i, i + 1) for i in range(peers -...]
    reshape x5 -> x0, local copies, waits for them, and re-layouts: 3.39 us -> none  [the longest x1 2.31 us: local(): cotangent.reshape(peers, capacity, down_width, 64)]
    unnamed x20 -> x8, local copies, waits for them, and re-layouts: 8.45 us -> 5.44 us
  transfers between devices with their start and end apart: 5 -> 0, of which waited for: 1 -> 0; matrix products, arithmetic and copies ran while one was open for 4% -> 0% of each run, Pallas kernels for 4% -> 0%
where the time goes in v2:
time: 60.5 us; the launch traced here: 60.3 us
  Pallas kernels  54.2 us (90%)
  local copies, waits for them, and re-layouts  5.44 us (9%)
  between operations  0.65 us (1%)
    pallas_call x1, Pallas kernels, local(): pl.pallas_call(step_kernel, out_shape=(jax.ShapeDtypeStruct(cotangent.sha...  54.2 us
    unnamed x8, local copies, waits for them, and re-layouts  5.44 us

profile of v2, /device:TPU:1, one launch (start us, length us, event | category | flops | bytes accessed | tf_op | source)
XLA Modules:
  0.0 60.3 jit_solution(11347055206050061778)
XLA Ops:
  0.6 1.3 %copy.10.owner = s32[8,1]{1,0:T(8,128)} copy(s32[8,1]{0,1:T(1,128)} %param.12) | data formatting | bytes 64 | tf_op args[5]
  2.0 54.2 %shard_map.94 = (bf16[64,64,64]{2,1,0:T(8,128)(2,1)}, f32[27,32,128]{2,1,0:T(8,128)}, f32[8,64,128]{2,1,0:T(8,128)}) custom-call(s32[8,26]{1,0:T(8,128)} %near.1, s32[8,1]{1,0:T(8,128)} %copy.10.owner, bf16[8,128,512]{2,1,0:T(8,128)(2,1)} %features_hbm.1, s32[8,512]{1,0:T(8,128)} %mask_hbm.1, bf16[27,32,128]{2,1,0:T(8,128)(2,1)} %w_conv_hbm.1, ...), custom_call_target="tpu_custom_call" | custom-call | tf_op jit(solution)/shard_map/pallas_call | solution.py:555
  56.2 0.0 copy-start
  56.2 2.3 %copy.14 = bf16[64,64,64]{2,1,0:T(8,128)(2,1)} copy(bf16[64,64,64]{2,1,0:T(8,128)(2,1)} %get-tuple-element.6) | data formatting | bytes 1048576
  58.5 0.0 copy-done
  58.5 0.0 copy-start.1
  58.5 0.8 %copy.15 = f32[27,32,128]{2,1,0:T(8,128)} copy(f32[27,32,128]{2,1,0:T(8,128)S(1)} %copy-done) | data formatting | bytes 884736
  59.2 0.3 copy-done.1
  59.6 0.7 %copy.16 = f32[8,64,128]{2,1,0:T(8,128)} copy(f32[8,64,128]{2,1,0:T(8,128)S(1)} %copy-done.1) | data formatting | bytes 524288
Async XLA Ops:
  56.2 2.3 %copy-start = (f32[27,32,128]{2,1,0:T(8,128)S(1)}, f32[27,32,128]{2,1,0:T(8,128)}, u32[]{:S(2)}) copy-start(f32[27,32,128]{2,1,0:T(8,128)} %get-tuple-element.7) | copy-start | bytes 1327108
  58.5 1.1 %copy-start.1 = (f32[8,64,128]{2,1,0:T(8,128)S(1)}, f32[8,64,128]{2,1,0:T(8,128)}, u32[]{:S(2)}) copy-start(f32[8,64,128]{2,1,0:T(8,128)} %get-tuple-element.8) | copy-start | bytes 786436

commit v3 on v2

--- a/solution.py
+++ b/solution.py
@@ -114,6 +114,19 @@
     return lax.rem(place + step, count)
 
 
+HALF = (256, 128, 128, 256)
+FULL = (256, 128, 128, 192)
+LEAD = ("z", "x", "y", "z")
+CONV_ROWS = [(3, 32 * k + (64 if k > 5 else 0)) for k in range(11)]
+CONV_ROWS += [(1, 32 * k) for k in range(8)] + [(2, 32 * k) for k in range(8)]
+
+
+def group_of(color, ny, nx, nz):
+    return {
+        "z": (("y", ny), ("x", nx)), "x": (("z", nz), ("y", ny)), "y": (("z", nz), ("x", nx)),
+    }[LEAD[color]]
+
+
 class Reduce:
     def __init__(self, links, grads, pair, first, rest, second, sums, sems):
         self.k = links
@@ -121,11 +134,9 @@
         self.second, self.sums, self.sems = second, sums, sems
         self.partner = links.device(core=1 - links.core)
         k = links
-        self.major = [("z", k.nz), ("x", k.nx), ("y", k.ny)]
-        self.minor = [
-            (("y", k.ny), ("x", k.nx)), (("z", k.nz), ("y", k.ny)), (("z", k.nz), ("x", k.nx)),
-        ]
-        self.cell = 256 // (k.nx * k.ny)
+        self.counts = {"z": k.nz, "x": k.nx, "y": k.ny}
+        self.minor = [group_of(color, k.ny, k.nx, k.nz) for color in range(4)]
+        self.cell = [half // (k.nx * k.ny) for half in HALF]
 
     def at(self, name):
         return getattr(self.k, name)
@@ -134,47 +145,50 @@
         return (self.sems.at[0, phase, color], self.sems.at[1, phase, color])
 
     def start_pair(self, color):
-        away = pl.multiple_of(256 * (1 - self.k.core), 256)
+        away = pl.multiple_of(HALF[color] * (1 - self.k.core), 128)
         send(
-            self.grads.at[color, :, pl.ds(away, 256)], self.pair.at[color],
-            self.sem(0, color), self.partner,
+            self.grads.at[color, :, pl.ds(away, FULL[color])],
+            self.pair.at[color, :, 0 : FULL[color]], self.sem(0, color), self.partner,
         )
 
     def part(self, color, place):
-        half = 256 * self.k.core
-        if color == 0:
-            return self.grads.at[color, place, pl.ds(pl.multiple_of(half, 256), 256)]
-        rows = 256 // self.major[color][1]
-        return self.grads.at[color, :, pl.ds(pl.multiple_of(half + place * rows, rows), rows)]
+        base = HALF[color] * self.k.core
+        if LEAD[color] == "z":
+            return place, pl.ds(pl.multiple_of(base, 128), FULL[color])
+        rows = HALF[color] // self.counts[LEAD[color]]
+        return slice(None), pl.ds(pl.multiple_of(base + place * rows, rows), rows)
 
     def start_major(self, color):
-        half = pl.ds(pl.multiple_of(256 * self.k.core, 256), 256)
-        arrived(self.pair.at[color], self.sem(0, color), self.partner)
+        full = FULL[color]
+        rows = pl.ds(pl.multiple_of(HALF[color] * self.k.core, 128), full)
+        arrived(self.pair.at[color, :, 0:full], self.sem(0, color), self.partner)
         for z in range(self.k.nz):
-            self.grads[color, z, half] += self.pair[color, z]
-        name, count = self.major[color]
+            self.grads[color, z, rows] += self.pair[color, z, 0:full]
+        name = LEAD[color]
+        count = self.counts[name]
         for step in range(1, count):
             place = shifted(self.at(name), step, count)
+            chunk, span = self.part(color, place)
             send(
-                self.part(color, place), self.first[color].at[step - 1],
+                self.grads.at[color, chunk, span], self.first[color].at[step - 1],
                 self.sem(1, color), self.k.device(**{name: place}),
             )
 
     def start_minor(self, color):
-        name, count = self.major[color]
-        place = self.at(name)
+        name = LEAD[color]
+        count = self.counts[name]
         if count > 1:
             arrived(self.first[color].at[0 : count - 1], self.sem(1, color), self.partner)
-        half = 256 * self.k.core
-        if color == 0:
-            total = self.grads[0, place, pl.ds(pl.multiple_of(half, 256), 256)]
-        else:
-            rows = 256 // count
-            total = self.grads[color, :, pl.ds(pl.multiple_of(half + place * rows, rows), rows)]
+        chunk, span = self.part(color, self.at(name))
+        total = self.grads[color, chunk, span]
         for step in range(count - 1):
             total = total + self.first[color][step]
+        cell = self.cell[color]
+        used = FULL[color] // cell
+        if LEAD[color] != "z":
+            used = self.rest[color].shape[0]
+        self.rest[color][0:used] = total.reshape(used, cell, 128)
         (n0, c0), (n1, c1) = self.minor[color]
-        self.rest[color][...] = total.reshape(c0, c1, self.cell, 128)
         for step0 in range(c0):
             for step1 in range(c1):
                 if step0 == 0 and step1 == 0:
@@ -182,21 +196,23 @@
                 p0 = shifted(self.at(n0), step0, c0)
                 p1 = shifted(self.at(n1), step1, c1)
                 send(
-                    self.rest[color].at[p0, p1], self.second[color].at[step0 * c1 + step1 - 1],
+                    self.rest[color].at[p0 * c1 + p1],
+                    self.second[color].at[step0 * c1 + step1 - 1],
                     self.sem(2, color), self.k.device(**{n0: p0, n1: p1}),
                 )
 
     def home(self, color):
         k = self.k
-        inner = (k.x * k.ny + k.y) if color == 1 else (k.y * k.nx + k.x)
-        return pl.ds(pl.multiple_of(256 * k.core + inner * self.cell, self.cell), self.cell)
+        inner = (k.x * k.ny + k.y) if LEAD[color] == "x" else (k.y * k.nx + k.x)
+        cell = self.cell[color]
+        return pl.ds(pl.multiple_of(HALF[color] * k.core + inner * cell, cell), cell)
 
     def start_spread(self, color):
         k = self.k
         (n0, c0), (n1, c1) = self.minor[color]
         if c0 * c1 > 1:
             arrived(self.second[color], self.sem(2, color), self.partner)
-        total = self.rest[color][self.at(n0), self.at(n1)]
+        total = self.rest[color][self.at(n0) * c1 + self.at(n1)]
         for step in range(c0 * c1 - 1):
             total = total + self.second[color][step]
         self.sums[color, self.home(color)] = total
@@ -209,47 +225,49 @@
                 mine = self.sums.at[color, self.home(color)]
                 send(mine, mine, self.sem(3, color), k.device(y=y, x=x))
 
+    def others(self, color):
+        return self.sums.at[color, 0 : (self.k.nx * self.k.ny - 1) * self.cell[color]]
+
     def start_share(self, color):
-        k = self.k
-        others = k.nx * k.ny - 1
-        if others:
-            arrived(self.sums.at[color, 0 : others * self.cell], self.sem(3, color), self.partner)
-        half = pl.ds(pl.multiple_of(256 * k.core, 256), 256)
-        mine = self.sums.at[color, half]
+        if self.k.nx * self.k.ny > 1:
+            arrived(self.others(color), self.sem(3, color), self.partner)
+        half = HALF[color]
+        mine = self.sums.at[color, pl.ds(pl.multiple_of(half * self.k.core, 128), half)]
         send(mine, mine, self.sem(4, color), self.partner)
 
     def finish(self, color):
-        k = self.k
-        arrived(self.sums.at[color, 0:256], self.sem(4, color), self.partner)
-        left(self.pair.at[color], self.sem(0, color), self.partner)
-        count = self.major[color][1]
+        half = self.sums.at[color, 0 : HALF[color]]
+        arrived(half, self.sem(4, color), self.partner)
+        left(self.pair.at[color, :, 0 : FULL[color]], self.sem(0, color), self.partner)
+        count = self.counts[LEAD[color]]
         if count > 1:
             left(self.first[color].at[0 : count - 1], self.sem(1, color), self.partner)
         if self.minor[color][0][1] * self.minor[color][1][1] > 1:
             left(self.second[color], self.sem(2, color), self.partner)
-        others = k.nx * k.ny - 1
-        if others:
-            left(self.sums.at[color, 0 : others * self.cell], self.sem(3, color), self.partner)
-        left(self.sums.at[color, 0:256], self.sem(4, color), self.partner)
+        if self.k.nx * self.k.ny > 1:
+            left(self.others(color), self.sem(3, color), self.partner)
+        left(half, self.sem(4, color), self.partner)
 
 
 def reduce_scratch(peers, nz):
     ny, nx = grid_of(peers)
-    cell = 256 // (nx * ny)
+    counts = {"z": nz, "x": nx, "y": ny}
+    first, rest, second = [], [], []
+    for color in range(4):
+        count = counts[LEAD[color]]
+        if LEAD[color] == "z":
+            shape = (max(count - 1, 1), FULL[color], 128)
+        else:
+            shape = (max(count - 1, 1), nz, HALF[color] // count, 128)
+        first.append(pltpu.VMEM(shape, F32))
+        (_, c0), (_, c1) = group_of(color, ny, nx, nz)
+        cell = HALF[color] // (nx * ny)
+        rest.append(pltpu.VMEM((c0 * c1, cell, 128), F32))
+        second.append(pltpu.VMEM((max(c0 * c1 - 1, 1), cell, 128), F32))
     return [
-        pltpu.VMEM((3, nz, 512, 128), F32),
-        pltpu.VMEM((3, nz, 256, 128), F32),
-        pltpu.VMEM((nz - 1, 256, 128), F32),
-        pltpu.VMEM((max(nx - 1, 1), nz, 256 // nx, 128), F32),
-        pltpu.VMEM((max(ny - 1, 1), nz, 256 // ny, 128), F32),
-        pltpu.VMEM((ny, nx, cell, 128), F32),
-        pltpu.VMEM((nz, ny, cell, 128), F32),
-        pltpu.VMEM((nz, nx, cell, 128), F32),
-        pltpu.VMEM((max(ny * nx - 1, 1), cell, 128), F32),
-        pltpu.VMEM((nz * ny - 1, cell, 128), F32),
-        pltpu.VMEM((nz * nx - 1, cell, 128), F32),
-        pltpu.VMEM((3, 512, 128), F32),
-        pltpu.SemaphoreType.DMA((2, 5, 3)),
+        pltpu.VMEM((4, nz, 512, 128), F32), pltpu.VMEM((4, nz, 256, 128), F32),
+        *first, *rest, *second,
+        pltpu.VMEM((4, 512, 128), F32), pltpu.SemaphoreType.DMA((2, 5, 4)),
     ]
 
 
@@ -289,13 +307,13 @@
 
 def step_kernel(
     near, owner, features_hbm, mask_hbm, w_conv_hbm, w_down_hbm, cotangent_hbm,
-    coarse_hbm, conv_sum, down_sum,
+    coarse_hbm, conv_hbm, down_hbm,
     features, mask, w_own, w_down, cotangent, w_conv,
     table, rims, windows, octants, factor, slopes, row_mask,
     cot_out, cot_in, piece_out, piece_in, dpiece_out, dpiece_in,
-    halves, coarse_out, coarse_in, coarse, local_sems, front_sems,
-    grads, pair, first_z, first_x, first_y, rest_0, rest_1, rest_2,
-    second_0, second_1, second_2, sums, sems,
+    halves, coarse_out, coarse_in, local_sems, front_sems,
+    grads, pair, first_0, first_1, first_2, first_3, rest_0, rest_1, rest_2, rest_3,
+    second_0, second_1, second_2, second_3, sums, sems,
 ):
     links = Links()
     peers = links.ny * links.nx * 2
@@ -303,8 +321,8 @@
     partner = links.device(core=1 - links.core)
     mine = links.z * 2
     reduce = Reduce(
-        links, grads, pair, (first_z, first_x, first_y), (rest_0, rest_1, rest_2),
-        (second_0, second_1, second_2), sums, sems,
+        links, grads, pair, (first_0, first_1, first_2, first_3),
+        (rest_0, rest_1, rest_2, rest_3), (second_0, second_1, second_2, second_3), sums, sems,
     )
 
     def front(n):
@@ -329,8 +347,8 @@
     rims[1, 8:12] = jnp.zeros((4, 64, 128), BF16)
     rims[1, 16] = jnp.zeros((64, 128), BF16)
     for z in range(nz):
-        grads[1, z, 448:512] = jnp.zeros((64, 128), F32)
-        grads[2, z, 416:512] = jnp.zeros((96, 128), F32)
+        grads[3, z, 416:448] = jnp.zeros((32, 128), F32)
+    rest_3[...] = jnp.zeros_like(rest_3)
     for r in range(2):
         halves[r, 8] = jnp.zeros((64, 128), BF16)
     loads[0].wait()
@@ -406,6 +424,21 @@
     for b in range(2):
         fill_plane(windows, rims.at[0], near, b, mine, 0, -1)
         fill_plane(windows, rims.at[1], near, b, mine, 9, 1)
+    arrived(cot_in.at[0 : peers - 1], front(0), partner)
+    owners = [owner[0, g] for g in range(8)]
+    low = lax.broadcasted_iota(jnp.int32, (64, 128), 1) < 64
+    for z in range(4):
+        parts = []
+        for i in range(2):
+            g = 2 * z + i
+            rank = jnp.int32(0)
+            for h in range(g):
+                rank = rank + jnp.where(owners[h] == owners[g], 1, 0)
+            value = cot_in[owners[g]].astype(F32)
+            parts.append(jnp.where(rank == i, value, pltpu.roll(value, 64, 1)))
+        dpiece_out[z] = jnp.where(low, parts[0], parts[1]).astype(BF16)
+    start_columns(links, dpiece_out, dpiece_in, front(5))
+
     shared = w_conv.at[:, 0 : 16 * (nz - 1)]
     arrived(shared, front(3), partner)
 
@@ -434,41 +467,6 @@
     piece_out[...] = total.astype(BF16).reshape(nz, 64, 128)
     start_columns(links, piece_out, piece_in, front(4))
 
-    arrived(cot_in.at[0 : peers - 1], front(0), partner)
-    owners = [owner[g, 0] for g in range(8)]
-    low = lax.broadcasted_iota(jnp.int32, (64, 128), 1) < 64
-    for z in range(4):
-        parts = []
-        for i in range(2):
-            g = 2 * z + i
-            rank = jnp.int32(0)
-            for h in range(g):
-                rank = rank + jnp.where(owners[h] == owners[g], 1, 0)
-            value = cot_in[owners[g]].astype(F32)
-            parts.append(jnp.where(rank == i, value, pltpu.roll(value, 64, 1)))
-        dpiece_out[z] = jnp.where(low, parts[0], parts[1]).astype(BF16)
-    start_columns(links, dpiece_out, dpiece_in, front(5))
-
-    arrived(piece_in.at[0 : nz - 1], front(4), partner)
-    for g in range(8):
-        value = piece_in[g // 2].astype(F32)
-        swapped = pltpu.roll(value, 64, 1)
-        first, other = (value, swapped) if g % 2 == 0 else (swapped, value)
-        halves[0, g] = jnp.where(low, first, 0.0).astype(BF16)
-        halves[1, g] = jnp.where(low, 0.0, other).astype(BF16)
-
-    @pl.loop(0, peers)
-    def _(d):
-        place_0 = jnp.int32(8)
-        place_1 = jnp.int32(8)
-        for g in range(7, -1, -1):
-            hit = owners[g] == d
-            place_1 = jnp.where(hit, place_0, place_1)
-            place_0 = jnp.where(hit, g, place_0)
-        coarse_out[d] = halves[0, place_0] + halves[1, place_1]
-
-    start_exchange(links, coarse_out, coarse_in, front(9))
-
     arrived(dpiece_in.at[0 : nz - 1], front(5), partner)
     piece = dpiece_in[...].reshape(256, 128)
     piece_rows = piece.astype(F32).T.astype(BF16)
@@ -487,6 +485,26 @@
                 for qx in range(4):
                     row = 64 * (2 * qx + a) + 16 * t
                     slopes[b, row : row + 16, :] = dhidden[qx] * factor[b, row : row + 16, :]
+    arrived(piece_in.at[0 : nz - 1], front(4), partner)
+    for g in range(8):
+        value = piece_in[g // 2].astype(F32)
+        swapped = pltpu.roll(value, 64, 1)
+        first, other = (value, swapped) if g % 2 == 0 else (swapped, value)
+        halves[0, g] = jnp.where(low, first, 0.0).astype(BF16)
+        halves[1, g] = jnp.where(low, 0.0, other).astype(BF16)
+
+    @pl.loop(0, peers)
+    def _(d):
+        place_0 = jnp.int32(8)
+        place_1 = jnp.int32(8)
+        for g in range(7, -1, -1):
+            hit = owners[g] == d
+            place_1 = jnp.where(hit, place_0, place_1)
+            place_0 = jnp.where(hit, g, place_0)
+        coarse_out[d] = halves[0, place_0] + halves[1, place_1]
+
+    start_exchange(links, coarse_out, coarse_in, front(9))
+
     turned = [slopes[b].astype(BF16).astype(F32).T.astype(BF16) for b in range(2)]
     for dx in range(3):
         total = None
@@ -497,40 +515,46 @@
             total = part if total is None else total + part
         for d in range(9):
             k = 9 * dx + d
-            color, row = (1, 32 * k) if k < 14 else (2, 32 * (k - 14))
+            color, row = CONV_ROWS[k]
             for z in range(4):
                 grads[color, z, row : row + 32, :] = total[
                     32 * z : 32 * z + 32, 128 * d : 128 * d + 128
                 ]
         if dx == 0:
             reduce.start_major(0)
-        else:
-            reduce.start_pair(dx)
+        elif dx == 1:
+            reduce.start_pair(3)
+    reduce.start_pair(1)
+    reduce.start_pair(2)
+    reduce.start_major(3)
     reduce.start_major(1)
     reduce.start_major(2)
-    for color in range(3):
+    for color in (0, 1, 2, 3):
         reduce.start_minor(color)
-    for color in range(3):
+    for color in (0, 1, 2, 3):
         reduce.start_spread(color)
 
     arrived(coarse_in.at[0 : peers - 1], front(9), partner)
 
-    @pl.loop(0, peers)
-    def _(d):
-        coarse[2 * d] = coarse_in[d, :, 0:64]
-        coarse[2 * d + 1] = coarse_in[d, :, 64:128]
-
-    store = pltpu.make_async_copy(coarse, coarse_hbm, local_sems.at[5])
-    store.start()
-    for color in range(3):
+    stores = [pltpu.make_async_copy(coarse_in, coarse_hbm, local_sems.at[5])]
+    stores[0].start()
+    for color in (0, 1, 2, 3):
         reduce.start_share(color)
-    for color in range(3):
+    for color in range(4):
         reduce.finish(color)
-    for o in range(8):
-        down_sum[o] = sums[0, 64 * o : 64 * o + 64]
-    for k in range(27):
-        color, row = (1, 32 * k) if k < 14 else (2, 32 * (k - 14))
-        conv_sum[k] = sums[color, row : row + 32]
+        if color == 0:
+            for o in range(8):
+                pltpu.make_async_copy(
+                    sums.at[0, 64 * o : 64 * o + 64], down_hbm.at[o], local_sems.at[6]
+                ).start()
+        for k in range(27):
+            if CONV_ROWS[k][0] == color:
+                row = CONV_ROWS[k][1]
+                pltpu.make_async_copy(
+                    sums.at[color, row : row + 32], conv_hbm.at[k], local_sems.at[7]
+                ).start()
+    stores.append(pltpu.make_async_copy(down_hbm, down_hbm, local_sems.at[6]))
+    stores.append(pltpu.make_async_copy(conv_hbm, conv_hbm, local_sems.at[7]))
     left(cot_out.at[0 : peers - 1], front(0), partner)
     left(rims.at[0, 4:8], front(1), partner)
     left(rims.at[1, 0:4], front(2), partner)
@@ -543,24 +567,24 @@
             (front_sems.at[0, 5 + step], front_sems.at[1, 5 + step]), partner,
         )
     left(coarse_out.at[0 : peers - 1], front(9), partner)
-    store.wait()
+    for copy in stores:
+        copy.wait()
 
 
 def local(features, voxel_mask, neighbors, w_conv, w_down, coarse_owner, cotangent):
     peers = lax.axis_size("space")
     nz = lax.axis_size("chan")
-    vmem = pl.BlockSpec(memory_space=pltpu.VMEM)
     smem = pl.BlockSpec(memory_space=pltpu.SMEM)
     anywhere = pl.BlockSpec(memory_space=pl.ANY)
-    return pl.pallas_call(
+    coarse_pairs, conv_sum, down_sum = pl.pallas_call(
         step_kernel,
         out_shape=(
-            jax.ShapeDtypeStruct(cotangent.shape, BF16),
+            jax.ShapeDtypeStruct((peers, 64, 128), BF16),
             jax.ShapeDtypeStruct((27, 32, 128), F32),
             jax.ShapeDtypeStruct((8, 64, 128), F32),
         ),
         in_specs=[smem, smem] + [anywhere] * 5,
-        out_specs=(anywhere, vmem, vmem),
+        out_specs=(anywhere, anywhere, anywhere),
         scratch_shapes=[
             pltpu.VMEM((8, 128, 512), BF16),
             pltpu.VMEM((8, 512), jnp.int32),
@@ -584,15 +608,16 @@
             pltpu.VMEM((2, 9, 64, 128), BF16),
             pltpu.VMEM((peers, 64, 128), BF16),
             pltpu.VMEM((peers, 64, 128), BF16),
-            pltpu.VMEM(cotangent.shape, BF16),
-            pltpu.SemaphoreType.DMA((6,)),
+            pltpu.SemaphoreType.DMA((8,)),
             pltpu.SemaphoreType.DMA((2, 10)),
         ]
         + reduce_scratch(peers, nz),
         compiler_params=pltpu.CompilerParams(
             vmem_limit_bytes=56 << 20, collective_id=0, has_side_effects=True
         ),
-    )(neighbors, coarse_owner, features, voxel_mask, w_conv, w_down, cotangent)
+    )(neighbors, coarse_owner.reshape(1, 8), features, voxel_mask, w_conv, w_down, cotangent)
+    pairs = coarse_pairs.reshape(peers, 64, 2, 64).transpose(0, 2, 1, 3)
+    return (pairs.reshape(cotangent.shape), conv_sum, down_sum)
 
 
 def solution(mesh):

time: 60.5 us -> 58.4 us (0.965)
  local copies, waits for them, and re-layouts: 5.44 us -> 2.92 us
  other arithmetic: 0 us -> 1.23 us
  Pallas kernels: 54.2 us -> 53.4 us
    unnamed x8 -> x6, local copies, waits for them, and re-layouts: 5.44 us -> 1.47 us
    slice x0 -> x1, local copies, waits for them, and re-layouts: none -> 1.44 us
    concatenate x0 -> x1, other arithmetic: none -> 1.23 us
    pallas_call x1, Pallas kernels: 54.2 us -> 53.4 us  [local(): pl.pallas_call(step_kernel, out_shape=(jax.ShapeDtypeStruct((peers, 64, 1...]
where the time goes in v3:
time: 58.4 us; the launch traced here: 58.2 us
  Pallas kernels  53.4 us (91%)
  local copies, waits for them, and re-layouts  2.92 us (5%)
  other arithmetic  1.23 us (2%)
  between operations  0.67 us (1%)
    pallas_call x1, Pallas kernels, local(): pl.pallas_call(step_kernel, out_shape=(jax.ShapeDtypeStruct((peers, 64, 1...  53.4 us
    unnamed x6, local copies, waits for them, and re-layouts  1.47 us
    slice x1, local copies, waits for them, and re-layouts  1.44 us
    concatenate x1, other arithmetic  1.23 us

profile of v3, /device:TPU:1, one launch (start us, length us, event | category | flops | bytes accessed | tf_op | source)
XLA Modules:
  0.0 58.2 jit_solution(11227286171351381226)
XLA Ops:
  0.6 53.4 %shard_map.94 = (bf16[32,64,128]{2,1,0:T(8,128)(2,1)}, f32[27,32,128]{2,1,0:T(8,128)}, f32[8,64,128]{2,1,0:T(8,128)}) custom-call(s32[8,26]{1,0:T(8,128)} %near.1, s32[1,8]{1,0:T(1,128)} %bitcast.3, bf16[8,128,512]{2,1,0:T(8,128)(2,1)} %features_hbm.1, s32[8,512]{1,0:T(8,128)} %mask_hbm.1, bf16[27,32,128]{2,1,0:T(8,128)(2,1)} %w_conv_hbm.1, ...), custom_call_target="tpu_custom_call" | custom-call | tf_op jit(solution)/shard_map/pallas_call | solution.py:579
  54.1 1.4 %fusion = (bf16[32,64,64]{2,1,0:T(8,128)(2,1)S(1)}, bf16[32,64,64]{2,1,0:T(8,128)(2,1)S(1)}) fusion(bf16[32,64,128]{2,1,0:T(8,128)(2,1)} %get-tuple-element.6), kind=kLoop, calls=%fused_computation.1 | loop fusion | bytes 1048576 | tf_op jit(solution)/shard_map/slice
  55.5 0.0 copy-start
  55.5 0.0 copy-start.1
  55.5 1.2 %pad_maximum_fusion = bf16[32,128,64]{2,1,0:T(8,128)(2,1)} fusion(bf16[32,64,64]{2,1,0:T(8,128)(2,1)S(1)} %get-tuple-element.10, bf16[32,64,64]{2,1,0:T(8,128)(2,1)S(1)} %get-tuple-element.9), kind=kLoop, calls=%fused_computation | loop fusion | flops 1048576 | bytes 1048576 | tf_op jit(solution)/shard_map/concatenate
  56.8 0.0 copy-done
  56.8 0.8 %copy.12 = f32[27,32,128]{2,1,0:T(8,128)} copy(f32[27,32,128]{2,1,0:T(8,128)S(1)} %copy-done) | data formatting | bytes 884736
  57.5 0.0 copy-done.1
  57.5 0.7 %copy.13 = f32[8,64,128]{2,1,0:T(8,128)} copy(f32[8,64,128]{2,1,0:T(8,128)S(1)} %copy-done.1) | data formatting | bytes 524288
Async XLA Ops:
  55.5 1.3 %copy-start = (f32[27,32,128]{2,1,0:T(8,128)S(1)}, f32[27,32,128]{2,1,0:T(8,128)}, u32[]{:S(2)}) copy-start(f32[27,32,128]{2,1,0:T(8,128)} %get-tuple-element.15) | copy-start | bytes 1327108
  55.5 2.0 %copy-start.1 = (f32[8,64,128]{2,1,0:T(8,128)S(1)}, f32[8,64,128]{2,1,0:T(8,128)}, u32[]{:S(2)}) copy-start(f32[8,64,128]{2,1,0:T(8,128)} %get-tuple-element.16) | copy-start | bytes 786436

commit v4 on v3

--- a/solution.py
+++ b/solution.py
@@ -307,7 +307,7 @@
 
 def step_kernel(
     near, owner, features_hbm, mask_hbm, w_conv_hbm, w_down_hbm, cotangent_hbm,
-    coarse_hbm, conv_hbm, down_hbm,
+    coarse_pairs_ref, conv_ref, down_ref,
     features, mask, w_own, w_down, cotangent, w_conv,
     table, rims, windows, octants, factor, slopes, row_mask,
     cot_out, cot_in, piece_out, piece_in, dpiece_out, dpiece_in,
@@ -328,6 +328,14 @@
     def front(n):
         return (front_sems.at[0, n], front_sems.at[1, n])
 
+    def pass_on(dx):
+        for step in range(1, nz):
+            z = shifted(links.z, nz - step, nz)
+            rows = pl.ds(pl.multiple_of(32 * z + 16 * links.core, 16), 16)
+            piece = w_conv.at[dx, rows]
+            arrived(piece, front(10 + 3 * step + dx - 3), partner)
+            send(piece, piece, front(19 + dx), partner)
+
     loads = [
         pltpu.make_async_copy(source, target, local_sems.at[n])
         for n, (source, target) in enumerate(
@@ -364,14 +372,12 @@
         cot_out[d, :, 64:128] = cotangent[2 * d + 1]
 
     pl.semaphore_wait(barrier, signals)
-    for step in range(1, nz):
-        z = shifted(links.z, step, nz)
-        rows = pl.ds(pl.multiple_of(32 * links.z + 16 * links.core, 16), 16)
-        send(
-            w_conv.at[:, rows], w_conv.at[:, rows],
-            (front_sems.at[0, 5 + step], front_sems.at[1, 5 + step]), links.device(z=z),
-        )
-    start_exchange(links, cot_out, cot_in, front(0))
+    own_rows = pl.ds(pl.multiple_of(32 * links.z + 16 * links.core, 16), 16)
+    for dx in range(3):
+        for step in range(1, nz):
+            z = shifted(links.z, step, nz)
+            piece = w_conv.at[dx, own_rows]
+            send(piece, piece, front(10 + 3 * step + dx - 3), links.device(z=z))
 
     loads[2].wait()
     loads[3].wait()
@@ -393,6 +399,7 @@
         rims[1, j] = table[8 * j]
     send(rims.at[0, 4:8], rims.at[0, 8:12], front(1), following)
     send(rims.at[1, 0:4], rims.at[1, 12:16], front(2), previous)
+    start_exchange(links, cot_out, cot_in, front(0))
     for b in range(2):
         keep = mask[pl.ds(mine + b, 1), :].astype(F32)
         for h in range(2):
@@ -404,12 +411,7 @@
         def _(xp):
             fill_plane(windows, table, near, b, mine, xp, 0)
 
-    for step in range(1, nz):
-        z = shifted(links.z, nz - step, nz)
-        rows = pl.ds(pl.multiple_of(32 * z + 16 * links.core, 16), 16)
-        piece = w_conv.at[:, rows]
-        arrived(piece, (front_sems.at[0, 5 + step], front_sems.at[1, 5 + step]), partner)
-        send(piece, piece, front(3), partner)
+    pass_on(0)
     arrived(rims.at[0, 8:12], front(1), previous)
     arrived(rims.at[1, 12:16], front(2), following)
 
@@ -424,34 +426,38 @@
     for b in range(2):
         fill_plane(windows, rims.at[0], near, b, mine, 0, -1)
         fill_plane(windows, rims.at[1], near, b, mine, 9, 1)
-    arrived(cot_in.at[0 : peers - 1], front(0), partner)
-    owners = [owner[0, g] for g in range(8)]
-    low = lax.broadcasted_iota(jnp.int32, (64, 128), 1) < 64
-    for z in range(4):
-        parts = []
-        for i in range(2):
-            g = 2 * z + i
-            rank = jnp.int32(0)
-            for h in range(g):
-                rank = rank + jnp.where(owners[h] == owners[g], 1, 0)
-            value = cot_in[owners[g]].astype(F32)
-            parts.append(jnp.where(rank == i, value, pltpu.roll(value, 64, 1)))
-        dpiece_out[z] = jnp.where(low, parts[0], parts[1]).astype(BF16)
-    start_columns(links, dpiece_out, dpiece_in, front(5))
-
-    shared = w_conv.at[:, 0 : 16 * (nz - 1)]
-    arrived(shared, front(3), partner)
-
-    for b in range(2):
-        total = None
-        for dx in range(3):
+    for dx in range(3):
+        if dx < 2:
+            pass_on(dx + 1)
+        else:
+            arrived(cot_in.at[0 : peers - 1], front(0), partner)
+            owners = [owner[0, g] for g in range(8)]
+            low = lax.broadcasted_iota(jnp.int32, (64, 128), 1) < 64
+            for z in range(4):
+                parts = []
+                for i in range(2):
+                    g = 2 * z + i
+                    rank = jnp.int32(0)
+                    for h in range(g):
+                        rank = rank + jnp.where(owners[h] == owners[g], 1, 0)
+                    value = cot_in[owners[g]].astype(F32)
+                    parts.append(jnp.where(rank == i, value, pltpu.roll(value, 64, 1)))
+                dpiece_out[z] = jnp.where(low, parts[0], parts[1]).astype(BF16)
+            start_columns(links, dpiece_out, dpiece_in, front(5))
+
+        arrived(w_conv.at[dx, 0 : 16 * (nz - 1)], front(19 + dx), partner)
+        for b in range(2):
             part = lax.dot_general(
                 windows[b, dx : dx + 8].reshape(512, 1152), w_conv[dx], NT,
                 preferred_element_type=F32,
             )
-            total = part if total is None else total + part
+            if dx == 0:
+                slopes[b] = part
+            else:
+                slopes[b] += part
+    for b in range(2):
         own = table[pl.ds(8 * (mine + b), 8)].astype(F32).reshape(512, 128)
-        pre = own + total
+        pre = own + slopes[b]
         keep = row_mask[b]
         gate = jax.nn.sigmoid(pre)
         hidden = (keep * (pre * gate)).astype(BF16).reshape(4, 2, 4, 16, 128)
@@ -536,55 +542,66 @@
 
     arrived(coarse_in.at[0 : peers - 1], front(9), partner)
 
-    stores = [pltpu.make_async_copy(coarse_in, coarse_hbm, local_sems.at[5])]
-    stores[0].start()
+    coarse_pairs_ref[...] = coarse_in[...]
     for color in (0, 1, 2, 3):
         reduce.start_share(color)
     for color in range(4):
         reduce.finish(color)
         if color == 0:
             for o in range(8):
-                pltpu.make_async_copy(
-                    sums.at[0, 64 * o : 64 * o + 64], down_hbm.at[o], local_sems.at[6]
-                ).start()
+                down_ref[o] = sums[0, 64 * o : 64 * o + 64]
         for k in range(27):
             if CONV_ROWS[k][0] == color:
-                row = CONV_ROWS[k][1]
-                pltpu.make_async_copy(
-                    sums.at[color, row : row + 32], conv_hbm.at[k], local_sems.at[7]
-                ).start()
-    stores.append(pltpu.make_async_copy(down_hbm, down_hbm, local_sems.at[6]))
-    stores.append(pltpu.make_async_copy(conv_hbm, conv_hbm, local_sems.at[7]))
+                conv_ref[k] = sums[color, CONV_ROWS[k][1] : CONV_ROWS[k][1] + 32]
     left(cot_out.at[0 : peers - 1], front(0), partner)
     left(rims.at[0, 4:8], front(1), partner)
     left(rims.at[1, 0:4], front(2), partner)
-    left(shared, front(3), partner)
     left(piece_out.at[0 : nz - 1], front(4), partner)
     left(dpiece_out.at[0 : nz - 1], front(5), partner)
-    for step in range(1, nz):
-        left(
-            w_conv.at[:, 0:16],
-            (front_sems.at[0, 5 + step], front_sems.at[1, 5 + step]), partner,
+    for dx in range(3):
+        left(w_conv.at[dx, 0 : 16 * (nz - 1)], front(19 + dx), partner)
+        for step in range(1, nz):
+            left(w_conv.at[dx, 0:16], front(10 + 3 * step + dx - 3), partner)
+    left(coarse_out.at[0 : peers - 1], front(9), partner)
+
+
+def finish_kernel(pairs, conv, down, coarse_out, conv_out, down_out, coarse, sems):
+    quarter = pairs.shape[0] // 4
+    stores = [
+        pltpu.make_async_copy(conv, conv_out, sems.at[4]),
+        pltpu.make_async_copy(down, down_out, sems.at[5]),
+    ]
+    for store in stores:
+        store.start()
+    for n in range(4):
+        for d in range(n * quarter, (n + 1) * quarter):
+            coarse[2 * d] = pairs[d, :, 0:64]
+            coarse[2 * d + 1] = pairs[d, :, 64:128]
+        store = pltpu.make_async_copy(
+            coarse.at[2 * n * quarter : 2 * (n + 1) * quarter],
+            coarse_out.at[2 * n * quarter : 2 * (n + 1) * quarter], sems.at[n],
         )
-    left(coarse_out.at[0 : peers - 1], front(9), partner)
-    for copy in stores:
-        copy.wait()
+        store.start()
+        stores.append(store)
+    for store in stores:
+        store.wait()
 
 
 def local(features, voxel_mask, neighbors, w_conv, w_down, coarse_owner, cotangent):
     peers = lax.axis_size("space")
     nz = lax.axis_size("chan")
     smem = pl.BlockSpec(memory_space=pltpu.SMEM)
+    vmem = pl.BlockSpec(memory_space=pltpu.VMEM)
     anywhere = pl.BlockSpec(memory_space=pl.ANY)
     coarse_pairs, conv_sum, down_sum = pl.pallas_call(
         step_kernel,
         out_shape=(
-            jax.ShapeDtypeStruct((peers, 64, 128), BF16),
-            jax.ShapeDtypeStruct((27, 32, 128), F32),
-            jax.ShapeDtypeStruct((8, 64, 128), F32),
+            pltpu.VMEM((peers, 64, 128), BF16),
+            pltpu.VMEM((27, 32, 128), F32),
+            pltpu.VMEM((8, 64, 128), F32),
         ),
         in_specs=[smem, smem] + [anywhere] * 5,
-        out_specs=(anywhere, anywhere, anywhere),
+        out_specs=(vmem, vmem, vmem),
         scratch_shapes=[
             pltpu.VMEM((8, 128, 512), BF16),
             pltpu.VMEM((8, 512), jnp.int32),
@@ -609,15 +626,31 @@
             pltpu.VMEM((peers, 64, 128), BF16),
             pltpu.VMEM((peers, 64, 128), BF16),
             pltpu.SemaphoreType.DMA((8,)),
-            pltpu.SemaphoreType.DMA((2, 10)),
+            pltpu.SemaphoreType.DMA((2, 22)),
         ]
         + reduce_scratch(peers, nz),
         compiler_params=pltpu.CompilerParams(
             vmem_limit_bytes=56 << 20, collective_id=0, has_side_effects=True
         ),
     )(neighbors, coarse_owner.reshape(1, 8), features, voxel_mask, w_conv, w_down, cotangent)
-    pairs = coarse_pairs.reshape(peers, 64, 2, 64).transpose(0, 2, 1, 3)
-    return (pairs.reshape(cotangent.shape), conv_sum, down_sum)
+    return pl.pallas_call(
+        finish_kernel,
+        out_shape=(
+            jax.ShapeDtypeStruct(cotangent.shape, BF16),
+            jax.ShapeDtypeStruct((27, 32, 128), F32),
+            jax.ShapeDtypeStruct((8, 64, 128), F32),
+        ),
+        in_specs=[vmem] * 3,
+        out_specs=(anywhere,) * 3,
+        scratch_shapes=[
+            pltpu.VMEM(cotangent.shape, BF16), pltpu.SemaphoreType.DMA((6,)),
+        ],
+    )(
+        *(
+            pltpu.with_memory_space_constraint(value, pltpu.VMEM)
+            for value in (coarse_pairs, conv_sum, down_sum)
+        )
+    )
 
 
 def solution(mesh):

time: 58.4 us -> 55 us (0.942)
  local copies, waits for them, and re-layouts: 2.92 us -> 0 us
  other arithmetic: 1.23 us -> 0 us
  Pallas kernels: 53.4 us -> 54.2 us
    unnamed x6 -> x0, local copies, waits for them, and re-layouts: 1.47 us -> none
    slice x1 -> x0, local copies, waits for them, and re-layouts: 1.44 us -> none
    concatenate x1 -> x0, other arithmetic: 1.23 us -> none
    pallas_call x1 -> x2, Pallas kernels: 53.4 us -> 54.2 us  [the longest x1 52.9 us: local(): pl.pallas_call(step_kernel, out_shape=(pltpu.VMEM((peers, 64, 128), BF16)...]
where the time goes in v4:
time: 55 us; the launch traced here: 54.8 us
  Pallas kernels  54.2 us (99%)
  between operations  0.64 us (1%)
    pallas_call x1, Pallas kernels, local(): pl.pallas_call(step_kernel, out_shape=(pltpu.VMEM((peers, 64, 128), BF16)...  52.9 us
    pallas_call x1, Pallas kernels, local(): pl.pallas_call(finish_kernel, out_shape=(jax.ShapeDtypeStruct(cotangent.s...  1.27 us

profile of v4, /device:TPU:1, one launch (start us, length us, event | category | flops | bytes accessed | tf_op | source)
XLA Modules:
  0.0 54.8 jit_solution(2655549433807962936)
XLA Ops:
  0.6 52.9 %shard_map.94 = (bf16[32,64,128]{2,1,0:T(8,128)(2,1)S(1)}, f32[27,32,128]{2,1,0:T(8,128)S(1)}, f32[8,64,128]{2,1,0:T(8,128)S(1)}) custom-call(s32[8,26]{1,0:T(8,128)} %near.1, s32[1,8]{1,0:T(1,128)} %bitcast.1, bf16[8,128,512]{2,1,0:T(8,128)(2,1)} %features_hbm.1, s32[8,512]{1,0:T(8,128)} %mask_hbm.1, bf16[27,32,128]{2,1,0:T(8,128)(2,1)} %w_conv_hbm.1, ...), custom_call_target="tpu_custom_call" | custom-call | tf_op jit(solution)/shard_map/pallas_call | solution.py:596
  53.5 1.3 %shard_map.95 = (bf16[64,64,64]{2,1,0:T(8,128)(2,1)}, f32[27,32,128]{2,1,0:T(8,128)}, f32[8,64,128]{2,1,0:T(8,128)}) custom-call(bf16[32,64,128]{2,1,0:T(8,128)(2,1)S(1)} %get-tuple-element.6.pairs, f32[27,32,128]{2,1,0:T(8,128)S(1)} %get-tuple-element.7.conv, f32[8,64,128]{2,1,0:T(8,128)S(1)} %get-tuple-element.8.down), custom_call_target="tpu_custom_call" | custom-call | tf_op jit(solution)/shard_map/pallas_call | solution.py:636

commit v5 on v4

--- a/solution.py
+++ b/solution.py
@@ -371,6 +371,19 @@
         cot_out[d, :, 0:64] = cotangent[2 * d]
         cot_out[d, :, 64:128] = cotangent[2 * d + 1]
 
+    loads[2].wait()
+    loads[3].wait()
+
+    @pl.loop(0, 4)
+    def _(g):
+        keep = mask[pl.ds(g, 1), :].astype(F32).astype(BF16)
+        masked = features[g] * keep
+        for h in range(2):
+            turned = lax.dot_general(
+                order, masked[:, 256 * h : 256 * h + 256], NT, preferred_element_type=F32
+            )
+            table[pl.ds(8 * g + 4 * h, 4)] = turned.astype(BF16).reshape(4, 64, 128)
+
     pl.semaphore_wait(barrier, signals)
     own_rows = pl.ds(pl.multiple_of(32 * links.z + 16 * links.core, 16), 16)
     for dx in range(3):
@@ -379,10 +392,8 @@
             piece = w_conv.at[dx, own_rows]
             send(piece, piece, front(10 + 3 * step + dx - 3), links.device(z=z))
 
-    loads[2].wait()
-    loads[3].wait()
-
-    @pl.loop(0, 8)
+
+    @pl.loop(4, 8)
     def _(g):
         keep = mask[pl.ds(g, 1), :].astype(F32).astype(BF16)
         masked = features[g] * keep

time: 55 us -> 54.3 us (0.987)
  Pallas kernels: 54.2 us -> 53.5 us
    pallas_call x1, Pallas kernels: 52.9 us -> 52.2 us  [local(): pl.pallas_call(step_kernel, out_shape=(pltpu.VMEM((peers, 64, 128), BF16)...]
where the time goes in v5:
time: 54.3 us; the launch traced here: 54.2 us
  Pallas kernels  53.5 us (99%)
  between operations  0.64 us (1%)
    pallas_call x1, Pallas kernels, local(): pl.pallas_call(step_kernel, out_shape=(pltpu.VMEM((peers, 64, 128), BF16)...  52.2 us
    pallas_call x1, Pallas kernels, local(): pl.pallas_call(finish_kernel, out_shape=(jax.ShapeDtypeStruct(cotangent.s...  1.27 us

profile of v5, /device:TPU:1, one launch (start us, length us, event | category | flops | bytes accessed | tf_op | source)
XLA Modules:
  0.0 54.2 jit_solution(11677085293905793767)
XLA Ops:
  0.6 52.2 %shard_map.94 = (bf16[32,64,128]{2,1,0:T(8,128)(2,1)S(1)}, f32[27,32,128]{2,1,0:T(8,128)S(1)}, f32[8,64,128]{2,1,0:T(8,128)S(1)}) custom-call(s32[8,26]{1,0:T(8,128)} %near.1, s32[1,8]{1,0:T(1,128)} %bitcast.1, bf16[8,128,512]{2,1,0:T(8,128)(2,1)} %features_hbm.1, s32[8,512]{1,0:T(8,128)} %mask_hbm.1, bf16[27,32,128]{2,1,0:T(8,128)(2,1)} %w_conv_hbm.1, ...), custom_call_target="tpu_custom_call" | custom-call | tf_op jit(solution)/shard_map/pallas_call | solution.py:607
  52.9 1.3 %shard_map.95 = (bf16[64,64,64]{2,1,0:T(8,128)(2,1)}, f32[27,32,128]{2,1,0:T(8,128)}, f32[8,64,128]{2,1,0:T(8,128)}) custom-call(bf16[32,64,128]{2,1,0:T(8,128)(2,1)S(1)} %get-tuple-element.6.pairs, f32[27,32,128]{2,1,0:T(8,128)S(1)} %get-tuple-element.7.conv, f32[8,64,128]{2,1,0:T(8,128)S(1)} %get-tuple-element.8.down), custom_call_target="tpu_custom_call" | custom-call | tf_op jit(solution)/shard_map/pallas_call | solution.py:647

commit v6 on v5

--- a/solution.py
+++ b/solution.py
@@ -487,11 +487,6 @@
     arrived(dpiece_in.at[0 : nz - 1], front(5), partner)
     piece = dpiece_in[...].reshape(256, 128)
     piece_rows = piece.astype(F32).T.astype(BF16)
-    for o in range(8):
-        part = jnp.dot(piece, octants[o], preferred_element_type=F32)
-        for z in range(4):
-            grads[0, z, 64 * o : 64 * o + 64, :] = part[64 * z : 64 * z + 64]
-    reduce.start_pair(0)
     for b in range(2):
         for a in range(2):
             for t in range(4):
@@ -502,6 +497,11 @@
                 for qx in range(4):
                     row = 64 * (2 * qx + a) + 16 * t
                     slopes[b, row : row + 16, :] = dhidden[qx] * factor[b, row : row + 16, :]
+    for o in range(8):
+        part = jnp.dot(piece, octants[o], preferred_element_type=F32)
+        for z in range(4):
+            grads[0, z, 64 * o : 64 * o + 64, :] = part[64 * z : 64 * z + 64]
+    reduce.start_pair(0)
     arrived(piece_in.at[0 : nz - 1], front(4), partner)
     for g in range(8):
         value = piece_in[g // 2].astype(F32)

time: 54.3 us -> 54.7 us (level)
  no operation moved by 1% of the time
where the time goes in v6:
time: 54.7 us; the launch traced here: 54.5 us
  Pallas kernels  53.8 us (98%)
  between operations  0.64 us (1%)
    pallas_call x1, Pallas kernels, local(): pl.pallas_call(step_kernel, out_shape=(pltpu.VMEM((peers, 64, 128), BF16)...  52.6 us
    pallas_call x1, Pallas kernels, local(): pl.pallas_call(finish_kernel, out_shape=(jax.ShapeDtypeStruct(cotangent.s...  1.27 us

profile of v6, /device:TPU:1, one launch (start us, length us, event | category | flops | bytes accessed | tf_op | source)
XLA Modules:
  0.0 54.5 jit_solution(9554626353634129294)
XLA Ops:
  0.6 52.6 %shard_map.94 = (bf16[32,64,128]{2,1,0:T(8,128)(2,1)S(1)}, f32[27,32,128]{2,1,0:T(8,128)S(1)}, f32[8,64,128]{2,1,0:T(8,128)S(1)}) custom-call(s32[8,26]{1,0:T(8,128)} %near.1, s32[1,8]{1,0:T(1,128)} %bitcast.1, bf16[8,128,512]{2,1,0:T(8,128)(2,1)} %features_hbm.1, s32[8,512]{1,0:T(8,128)} %mask_hbm.1, bf16[27,32,128]{2,1,0:T(8,128)(2,1)} %w_conv_hbm.1, ...), custom_call_target="tpu_custom_call" | custom-call | tf_op jit(solution)/shard_map/pallas_call | solution.py:607
  53.2 1.3 %shard_map.95 = (bf16[64,64,64]{2,1,0:T(8,128)(2,1)}, f32[27,32,128]{2,1,0:T(8,128)}, f32[8,64,128]{2,1,0:T(8,128)}) custom-call(bf16[32,64,128]{2,1,0:T(8,128)(2,1)S(1)} %get-tuple-element.6.pairs, f32[27,32,128]{2,1,0:T(8,128)S(1)} %get-tuple-element.7.conv, f32[8,64,128]{2,1,0:T(8,128)S(1)} %get-tuple-element.8.down), custom_call_target="tpu_custom_call" | custom-call | tf_op jit(solution)/shard_map/pallas_call | solution.py:647
